TPU v7x, 256 devices: a whole 4x4x8 slice. The times are simulated.
256 devices in a mesh: dp: 16 (over y, x), cluster: 16 (over z, core).
Axes of the slice: x: 4, y: 4, z: 8, core: 2. Of those that a mesh axis runs over, the one named last changes fastest.
Arguments:
- points: bfloat16 [524288, 768], P(('dp', 'cluster')), may hold values from -12 to 12
- coarse_id: int32 [524288, 1], P(('dp', 'cluster')), may hold values from 0 to 255; in each aligned block of 2048 rows (0 to 2047, 2048 to 4095, ...) at most 24 rows name the same one
- owner_map: int32 [256], replicated, may hold values from 0 to 255, each once
- centroids: bfloat16 [256, 256, 768], P('cluster', 'dp'), may hold values from -1 to 1
Outputs:
- new_centroids: bfloat16 [256, 256, 768], P('cluster', 'dp')
- point_score: float32 [524288], P(('dp', 'cluster'))
Inputs may be any that keep to these rules, and one draw needn't show every extreme that they name: `coarse_id`: in the rows of one device no coarse cluster appears more than 24 times, and some cluster appears exactly 24 times. `owner_map`: a permutation; slot s lies on cluster index s // 16.
All inputs are finite; a program needn't handle non-finite values.
Results may differ from a plain program's by a relative error of at most 0.007.
Values may be sent and summed in bfloat16 or wider, within the bound.
No kernel may reach another device: no remote copies, remote signals or barrier semaphores. Data moves between devices by JAX's collectives and lax.ppermute only.
A program may use at most 128 MiB of HBM per device.

v0:
```python
import jax
import jax.numpy as jnp
from jax import lax
from jax.sharding import PartitionSpec as P

prior_mass = 4.0


def local(points, coarse_id, owner_map, centroids):
    slots_dev = centroids.shape[0]
    feature_width = points.shape[1]
    cluster_count = lax.axis_size("cluster")
    total_slots = owner_map.shape[0]
    point_rows = points.shape[0]
    capacity = 3 * point_rows // total_slots
    coarse = coarse_id[:, 0]
    slot_ids = jnp.arange(total_slots, dtype=jnp.int32)
    lookup = coarse[:, None] == slot_ids[None, :]
    slot_index = jnp.sum(jnp.where(lookup, owner_map[None, :], 0), axis=1)
    slot_hits = (slot_index[:, None] == slot_ids[None, :]).astype(jnp.int32)
    position_in = jnp.sum((jnp.cumsum(slot_hits, 0) - 1) * slot_hits, axis=1)
    placement = slot_index * capacity + position_in
    outbound = (
        jnp.zeros((total_slots * capacity, feature_width), jnp.bfloat16).at[placement].set(points)
    )
    filled = (
        jnp.zeros((total_slots * capacity,), jnp.bfloat16)
        .at[placement]
        .set(jnp.ones((point_rows,), jnp.bfloat16))
    )
    panels = lax.all_gather(centroids, "dp", axis=1, tiled=True)
    inbound, present = (
        lax.all_to_all(outbound, "cluster", split_axis=0, concat_axis=0, tiled=True),
        lax.all_to_all(filled, "cluster", split_axis=0, concat_axis=0, tiled=True),
    )
    arrived = inbound.reshape(cluster_count, slots_dev, capacity, feature_width)
    present_mask = present.reshape(cluster_count, slots_dev, capacity)
    sqnorm = jnp.sum(jnp.square(panels.astype(jnp.float32)), -1)
    logits = (
        jnp.einsum("sjcd,jfd->sjcf", arrived, panels, preferred_element_type=jnp.float32)
        - 0.5 * sqnorm[None, :, None, :]
    )
    row_peak = jnp.max(logits, -1, keepdims=True)
    shifted = jnp.exp(logits - row_peak)
    row_total = jnp.sum(shifted, -1, keepdims=True)
    log_total = row_peak[..., 0] + jnp.log(row_total[..., 0])
    weights_bf = (shifted / row_total).astype(jnp.bfloat16) * present_mask[..., None]
    returned = lax.all_to_all(
        log_total.reshape(-1), "cluster", split_axis=0, concat_axis=0, tiled=True
    )
    point_score = returned[placement]
    weighted = jnp.einsum("sjcf,sjcd->jfd", weights_bf, arrived, preferred_element_type=jnp.float32)
    counts = jnp.sum(weights_bf.astype(jnp.float32), axis=(0, 2))
    weighted_part, counts_part = (
        lax.psum_scatter(weighted, "dp", scatter_dimension=1, tiled=True),
        lax.psum_scatter(counts, "dp", scatter_dimension=1, tiled=True),
    )
    updated = (
        (weighted_part + prior_mass * centroids.astype(jnp.float32))
        / (counts_part[..., None] + prior_mass)
    ).astype(jnp.bfloat16)
    return (updated, point_score)


def solution(mesh):
    placed = (P(("dp", "cluster"), None), P(("dp", "cluster"), None), P(), P("cluster", "dp", None))
    return jax.shard_map(
        local,
        mesh=mesh,
        in_specs=placed,
        out_specs=(P("cluster", "dp", None), P(("dp", "cluster"))),
        check_vma=False,
    )
```

profile of v0, /device:TPU:2, one launch (start us, length us, event | category | flops | bytes accessed | tf_op | source)
XLA Modules:
  0.0 402.9 jit_solution(2727471434417005122)
XLA Ops:
  7.2 1.4 select_reduce_fusion
  8.6 0.1 copy.13
  8.7 0.3 fusion.14
  9.1 0.3 add_add_fusion
  9.4 1.2 copy.14
  10.6 0.9 fusion.13
  11.6 14.6 %scatter_custom_fusion.1 = bf16[6144]{0:T(1024)(128)(2,1)S(1)} fusion(s32[2048]{0:T(1024)S(1)} %bitcast.51, bf16[2048]{0:T(1024)(128)(2,1)S(1)} %broadcast.64, bf16[]{:T(256)} %constant.10.clone.1), kind=kCustom, calls=%fused_computation.36 | custom fusion | bytes 12290 | tf_op jit(solution)/shard_map/scatter | solution.py:29
  26.2 0.5 broadcast.74
  26.7 0.7 reduce.2
  27.4 0.7 reshape.130
  28.1 8.6 %all-to-all-start.1 = ((bf16[16,2,192]{2,1,0:T(2,128)(2,1)}), bf16[16,2,192]{2,1,0:T(2,128)(2,1)S(1)}, u32[]{:S(2)}, u32[]{:S(2)}) async-start(bf16[16,2,192]{2,1,0:T(2,128)(2,1)} %reshape.130), calls=%async_computation.1 | async-start | bytes 32768 | tf_op jit(solution)/shard_map/all_to_all | solution.py:34
  36.7 15.7 %scatter_custom_fusion = bf16[6144,768]{1,0:T(8,128)(2,1)} fusion(s32[2048]{0:T(1024)S(1)} %bitcast.52, bf16[2048,768]{1,0:T(8,128)(2,1)} %param.4, bf16[]{:T(256)} %constant.10.clone.1), kind=kCustom, calls=%fused_computation.15 | custom fusion | bytes 9437696 | tf_op jit(solution)/shard_map/scatter | solution.py:24
  52.4 0.0 all-to-all-done.1
  52.4 7.3 %all-to-all-start = ((bf16[16,384,768]{2,1,0:T(8,128)(2,1)}), bf16[16,384,768]{2,1,0:T(8,128)(2,1)}, u32[]{:S(2)}, u32[]{:S(2)}) async-start(bf16[16,384,768]{2,1,0:T(8,128)(2,1)} %bitcast.47), calls=%async_computation | async-start | bytes 18874368 | tf_op jit(solution)/shard_map/all_to_all | solution.py:33
  59.6 0.0 all-gather.2.cloned.1.call-start
  59.7 0.7 all-gather.2.cloned.1.call-update
  60.4 0.0 reduce-scatter.3.cloned.1.call-start
  60.4 0.1 reshape.131
  60.5 0.1 bitcast_reduce_fusion.1
  60.6 0.1 mul.49
  60.8 69.7 %all-gather.2.cloned.1.call-done = bf16[16,256,768]{2,1,0:T(8,128)(2,1)} async-done(((bf16[16,16,768]{2,1,0:T(8,128)(2,1)}), bf16[16,256,768]{2,1,0:T(8,128)(2,1)}) %all-gather.2.cloned.1.call-update) | async-done | bytes 6291472 | tf_op jit(solution)/shard_map/all_gather | solution.py:31
  130.4 4.1 %multiply_reduce_fusion = f32[16,256]{1,0:T(8,128)S(1)} fusion(bf16[16,256,768]{2,1,0:T(8,128)(2,1)} %all-gather.2.cloned.1.call-done), kind=kLoop, calls=%fused_computation.3 | loop fusion | flops 9433088 | bytes 6307840 | tf_op jit(solution)/shard_map/reduce_sum | solution.py:38
  134.5 131.8 %all-to-all-done = bf16[16,384,768]{2,1,0:T(8,128)(2,1)} async-done(((bf16[16,384,768]{2,1,0:T(8,128)(2,1)}), bf16[16,384,768]{2,1,0:T(8,128)(2,1)}, u32[]{:S(2)}, u32[]{:S(2)}) %all-to-all-start) | async-done | bytes 9437216 | tf_op jit(solution)/shard_map/all_to_all | solution.py:33
  266.3 10.8 %bitcast_reduce_fusion = (f32[16,16,24]{2,0,1:T(8,128)S(1)}, f32[16,16,24,256]{3,2,1,0:T(8,128)}) fusion(f32[16,256]{1,0:T(8,128)S(1)} %broadcast_multiply_fusion, bf16[16,256,768]{2,1,0:T(8,128)(2,1)} %all-gather.2.cloned.1.call-done, bf16[16,16,24,768]{3,2,1,0:T(8,128)(2,1)} %bitcast.8), kind=kOutput, calls=%fused_computation.10 | convolution fusion | flops 2419058688 | bytes 22061056 | tf_op jit(solution)/shard_map/sjcd,jfd->sjcf/dot_general | solution.py:40
  277.1 0.0 copy-start
  277.1 4.3 %fusion.6 = f32[16,16,24]{2,0,1:T(8,128)S(1)} fusion(f32[16,16,24,256]{3,2,1,0:T(8,128)} %get-tuple-element.5, f32[16,16,24]{2,0,1:T(8,128)S(1)} %get-tuple-element.4, f32[16,256]{1,0:T(8,128)S(1)} %broadcast_multiply_fusion), kind=kLoop, calls=%fused_computation.14 | loop fusion | flops 4712448 | bytes 6356992 | tf_op jit(solution)/shard_map/reduce_sum | solution.py:45
  281.4 0.3 copy-done
  281.8 3.1 convert_reduce_fusion
  284.9 10.1 %fusion.9 = f32[16,256,768]{2,1,0:T(8,128)} fusion(bf16[16,16,24,256]{3,2,0,1:T(8,128)(2,1)S(1)} %get-tuple-element.3, bf16[16,16,24,768]{3,2,1,0:T(8,128)(2,1)} %bitcast.8), kind=kOutput, calls=%fused_computation.17 | convolution fusion | flops 2415919104 | bytes 25165824 | tf_op jit(solution)/shard_map/sjcf,sjcd->jfd/dot_general | solution.py:52
  295.0 0.0 copy-start.2
  295.0 0.0 reduce-scatter.3.cloned.1.call-update
  295.0 0.0 copy-start.1
  295.0 0.6 copy-done.2
  295.7 0.6 dynamic-slice
  297.0 0.7 add.64
  297.7 4.7 %all-to-all-start.2 = ((f32[16,384,1]{1,2,0:T(1,128)}), f32[16,384,1]{1,2,0:T(1,128)S(1)}, u32[]{:S(2)}, u32[]{:S(2)}) async-start(f32[16,384,1]{1,2,0:T(1,128)} %add.64), calls=%async_computation.3 | async-start | bytes 49152 | tf_op jit(solution)/shard_map/all_to_all | solution.py:48
  302.5 70.8 %all-reduce = f32[16,256]{1,0:T(8,128)S(1)} all-reduce(f32[16,256]{1,0:T(8,128)S(1)} %get-tuple-element.2), channel_id=3, replica_groups=mesh['dp'=16,'cluster'=16] {'dp'}, use_global_device_ids=true, to_apply=%region_11.12.clone | all-reduce | flops 4096 | bytes 32768
  373.3 0.1 dynamic-slice_add_fusion
  373.4 0.0 all-to-all-done.2
  373.4 20.5 %gather_fusion = f32[2048]{0:T(1024)} fusion(f32[6144]{0:T(1024)S(1)} %bitcast.46, s32[2048]{0:T(1024)S(1)} %broadcast_clamp_fusion), kind=kCustom, calls=%fused_computation | custom fusion | bytes 24576 | tf_op jit(solution)/shard_map/gather | solution.py:51
  393.9 0.1 reduce-scatter.3.cloned.1.call-done
  394.0 0.0 copy-done.1
  394.0 2.0 divide_convert_fusion.1
  (12 shorter events, 0.2 us)
Async XLA Ops:
  28.1 24.3 %all-to-all-start.1 = ((bf16[16,2,192]{2,1,0:T(2,128)(2,1)}), bf16[16,2,192]{2,1,0:T(2,128)(2,1)S(1)}, u32[]{:S(2)}, u32[]{:S(2)}) async-start(bf16[16,2,192]{2,1,0:T(2,128)(2,1)} %reshape.130), calls=%async_computation.1 | async-start | bytes 32768 | tf_op jit(solution)/shard_map/all_to_all | solution.py:34
  52.4 213.9 %all-to-all-start = ((bf16[16,384,768]{2,1,0:T(8,128)(2,1)}), bf16[16,384,768]{2,1,0:T(8,128)(2,1)}, u32[]{:S(2)}, u32[]{:S(2)}) async-start(bf16[16,384,768]{2,1,0:T(8,128)(2,1)} %bitcast.47), calls=%async_computation | async-start | bytes 18874368 | tf_op jit(solution)/shard_map/all_to_all | solution.py:33
  59.6 70.8 %all-gather.2.cloned.1.call-start = ((), (), s32[]{:S(2)}) async-start(), calls=%async_computation.4 | async-start | bytes 6684672 | tf_op jit(solution)/shard_map/all_gather | solution.py:31
  60.4 333.7 %reduce-scatter.3.cloned.1.call-start = ((), (), s32[]{:S(2)}) async-start(), calls=%async_computation.5 | async-start | bytes 13369344 | tf_op jit(solution)/shard_map/reduce_scatter | solution.py:55
  277.1 4.6 %copy-start = (f32[16,16,24,256]{3,2,1,0:T(8,128)S(1)}, f32[16,16,24,256]{3,2,1,0:T(8,128)}, u32[]{:S(2)}) copy-start(f32[16,16,24,256]{3,2,1,0:T(8,128)} %get-tuple-element.5) | copy-start | bytes 18874372
  295.0 0.7 copy-start.2
  295.0 99.0 %copy-start.1 = (bf16[16,16,768]{2,1,0:T(8,128)(2,1)S(1)}, bf16[16,16,768]{2,1,0:T(8,128)(2,1)}, u32[]{:S(2)}) copy-start(bf16[16,16,768]{2,1,0:T(8,128)(2,1)} %param.7) | copy-start | bytes 1179652
  297.7 75.7 %all-to-all-start.2 = ((f32[16,384,1]{1,2,0:T(1,128)}), f32[16,384,1]{1,2,0:T(1,128)S(1)}, u32[]{:S(2)}, u32[]{:S(2)}) async-start(f32[16,384,1]{1,2,0:T(1,128)} %add.64), calls=%async_computation.3 | async-start | bytes 49152 | tf_op jit(solution)/shard_map/all_to_all | solution.py:48
Sparse Core Ops, SparseCore 0:
  62.9 67.4 all-gather.1
  295.1 98.8 reduce-scatter.2
where the time goes:
time: 408 us; the launch traced here: 403 us
  waiting for transfers between devices  202 us (50%)
  blocking collectives  70.8 us (17%)
  local copies, waits for them, and re-layouts  56.1 us (14%)
  matrix products  20.9 us (5%)
  starting transfers between devices  20.7 us (5%)
  other arithmetic  17.3 us (4%)
  between operations  14.9 us (4%)
    all_to_all x1, waiting for transfers between devices, local(): lax.all_to_all(outbound, 'cluster', split_axis=0, concat_axis=0, tiled=True)  132 us
    unnamed x1, blocking collectives  70.8 us
    all_gather x1, waiting for transfers between devices, local(): panels = lax.all_gather(centroids, 'dp', axis=1, tiled=True)  69.7 us
    gather x1, local copies, waits for them, and re-layouts, local(): point_score = returned[placement]  20.5 us
    scatter x1, local copies, waits for them, and re-layouts, local(): jnp.zeros((total_slots * capacity, feature_width), jnp.bfloat16)  15.7 us
    scatter x1, local copies, waits for them, and re-layouts, local(): filled = jnp.zeros((total_slots * capacity,), jnp.bfloat16).at[placement]...  14.6 us
    dot_general x1, matrix products, local(): jnp.einsum('sjcd,jfd->sjcf', arrived, panels, preferred_element_type=jnp....  10.8 us
    dot_general x1, matrix products, local(): jnp.einsum('sjcf,sjcd->jfd', weights_bf, arrived, preferred_element_type=...  10.1 us
  transfers between devices with their start and end apart: 5, of which 3 were waited for; matrix products, arithmetic and copies ran while one was open for 10% of the time, Pallas kernels for 0%

commit v1 on v0

v1 whole, which is shorter than its diff:
```python
import functools
import jax
import jax.numpy as jnp
from jax import lax
from jax.experimental import pallas as pl
from jax.experimental.pallas import tpu as pltpu
from jax.sharding import Mesh, PartitionSpec as P

PRIOR = 4.0
CAP = 24
ROWS = 128
PLANE = ("y", "x", "core")
BF = jnp.bfloat16
F32 = jnp.float32


def iota(shape, dim):
    return lax.broadcasted_iota(jnp.int32, shape, dim)


def dot(a, b, dims=((1,), (0,))):
    return lax.dot_general(a, b, (dims, ((), ())), preferred_element_type=F32)


def onehot(mask):
    return jnp.where(mask, 1.0, 0.0).astype(BF)


def index_kernel(zn, dpn, cores, bound, coarse_ref, owner_ref, place_ref, count_ref, hot_ref):
    slots = owner_ref.shape[1]
    rows = coarse_ref.shape[1]
    owner = owner_ref[...]
    column, cluster = owner % dpn, owner // dpn
    lane_of = (column * cores + cluster % cores) * zn + cluster // cores
    move = onehot(iota((slots, slots), 0) == lane_of)
    blk = 256
    earlier = onehot(iota((blk, blk), 0) < iota((blk, blk), 1))
    carry = jnp.zeros((slots, 1), F32)
    ranks = []
    for b in range(rows // blk):
        named = onehot(iota((slots, blk), 0) == coarse_ref[:, b * blk : (b + 1) * blk])
        hot = dot(move, named)
        hot_bf = hot.astype(BF)
        hot_ref[:, b * blk : (b + 1) * blk] = hot_bf
        before = dot(hot_bf, earlier) + carry
        ranks.append(jnp.sum(hot * before, axis=0, keepdims=True))
        carry = carry + jnp.sum(hot, axis=1, keepdims=True)
    rank = jnp.concatenate(ranks, axis=1)
    hot_all = hot_ref[...]
    counts = dot(jnp.ones((8, rows), BF), hot_all, ((1,), (1,)))
    la, lb = iota((slots, slots), 0), iota((slots, slots), 1)
    group = onehot((la // zn == lb // zn) & (la < lb))
    offset = dot(counts.astype(BF), group)
    which = iota((8, slots), 0)
    query = jnp.where(which == 0, offset, iota((8, slots), 1).astype(F32)).astype(BF)
    found = dot(query, hot_all)
    lane = found[1:2].astype(jnp.int32)
    rank = rank.astype(jnp.int32)
    pos = (lane // zn) * bound + found[0:1].astype(jnp.int32) + rank
    row = iota((8, rows), 0)
    place_ref[...] = jnp.where(row == 0, pos, jnp.where(row == 1, lane, rank))
    count_ref[...] = counts.astype(jnp.int32)


def index(coarse, owner, zn, dpn, cores, bound):
    rows, slots = coarse.shape[1], owner.shape[1]
    return pl.pallas_call(
        functools.partial(index_kernel, zn, dpn, cores, bound),
        out_shape=(
            jax.ShapeDtypeStruct((8, rows), jnp.int32),
            jax.ShapeDtypeStruct((8, slots), jnp.int32),
        ),
        scratch_shapes=[pltpu.VMEM((slots, rows), BF)],
        cost_estimate=pl.CostEstimate(flops=10**9, bytes_accessed=10**5, transcendentals=0),
        name="place",
    )(coarse, owner)


def pack_kernel(per, first, bound, place_ref, points_ref, out_ref):
    g = pl.program_id(0)
    tall = out_ref.shape[0]
    i = iota((tall, 1), 0)
    want = (g * (tall // per) + i // per) * bound + first + i % per
    pick = onehot(place_ref[0:1, :] == want)
    out_ref[...] = dot(pick, points_ref[...]).astype(BF)


def pack(place, points, peers, per, first, bound):
    rows, width = points.shape
    tall = 256
    return pl.pallas_call(
        functools.partial(pack_kernel, per, first, bound),
        grid=(peers * per // tall,),
        in_specs=[
            pl.BlockSpec((8, rows), lambda g: (0, 0)),
            pl.BlockSpec((rows, width), lambda g: (0, 0)),
        ],
        out_specs=pl.BlockSpec((tall, width), lambda g: (g, 0)),
        out_shape=jax.ShapeDtypeStruct((peers * per, width), BF),
        cost_estimate=pl.CostEstimate(
            flops=2 * peers * per * rows * width, bytes_accessed=10**7, transcendentals=0
        ),
        name="pack",
    )(place, points)


def assign_kernel(
    pairs, zn, flag_ref, dest_ref, more_dest_ref, live_ref, in_ref, more_ref, panel_ref,
    sums_ref, mass_ref, score_ref, held, more_vmem,
):
    g = pl.program_id(0)
    pad = 2 * CAP

    @pl.when(g < pairs)
    def _():
        tall = zn * pad
        pick = onehot(iota((tall, in_ref.shape[0]), 0) == dest_ref[pl.ds(g, 1), :])
        laid = dot(pick, in_ref[...]).astype(BF)
        start = pl.multiple_of(g * pad, 16)
        for j in range(zn):
            held[j, pl.ds(start, pad), :] = laid[j * pad : (j + 1) * pad]

        @pl.when(flag_ref[0] != 0)
        def _():
            deep = more_vmem.shape[0]
            pltpu.sync_copy(more_ref.at[pl.ds(pl.multiple_of(g * deep, deep), deep), :], more_vmem)
            pick = onehot(iota((tall, deep), 0) == more_dest_ref[pl.ds(g, 1), :])
            more = dot(pick, more_vmem[...])
            for j in range(zn):
                old = held[j, pl.ds(start, pad), :].astype(F32)
                held[j, pl.ds(start, pad), :] = (old + more[j * pad : (j + 1) * pad]).astype(BF)

    @pl.when(g >= pairs)
    def _():
        j = g - pairs
        x = held[j]
        panel = panel_ref[0]
        wide = panel.astype(F32)
        sqnorm = jnp.sum(wide * wide, axis=1, keepdims=True)
        logits = dot(panel, x, ((1,), (1,))) - 0.5 * sqnorm
        peak = jnp.max(logits, axis=0, keepdims=True)
        shifted = jnp.exp(logits - peak)
        total = jnp.sum(shifted, axis=0, keepdims=True)
        score_ref[pl.ds(j, 1), :] = peak + jnp.log(total)
        live = live_ref[pl.ds(j, 1), :]
        weights = jnp.where(live > 0, shifted * (1.0 / total), 0.0).astype(BF)
        sums_ref[0] = dot(weights, x).astype(BF)
        mass = dot(jnp.ones((8, x.shape[0]), BF), weights, ((1,), (1,)))
        mass_ref[pl.ds(j, 1), :] = mass[0:1]


def assign(flag, dest, more_dest, live, rows, more, panels):
    zn, fine, width = panels.shape
    pairs, deep = dest.shape
    more_deep = more_dest.shape[1]
    spread = pairs * 2 * CAP
    last = pairs - 1
    whole = lambda g, f: (0, 0)
    return pl.pallas_call(
        functools.partial(assign_kernel, pairs, zn),
        grid_spec=pltpu.PrefetchScalarGridSpec(
            num_scalar_prefetch=1,
            grid=(pairs + zn,),
            in_specs=[
                pl.BlockSpec((pairs, deep), whole),
                pl.BlockSpec((pairs, more_deep), whole),
                pl.BlockSpec((zn, spread), whole),
                pl.BlockSpec((deep, width), lambda g, f: (jnp.minimum(g, last), 0)),
                pl.BlockSpec(memory_space=pl.ANY),
                pl.BlockSpec((1, fine, width), lambda g, f: (jnp.maximum(g - pairs, 0), 0, 0)),
            ],
            out_specs=[
                pl.BlockSpec((1, fine, width), lambda g, f: (jnp.maximum(g - pairs, 0), 0, 0)),
                pl.BlockSpec((zn, fine), whole),
                pl.BlockSpec((zn, spread), whole),
            ],
            scratch_shapes=[
                pltpu.VMEM((zn, spread, width), BF),
                pltpu.VMEM((more_deep, width), BF),
            ],
        ),
        out_shape=(
            jax.ShapeDtypeStruct((zn, fine, width), BF),
            jax.ShapeDtypeStruct((zn, fine), F32),
            jax.ShapeDtypeStruct((zn, spread), F32),
        ),
        compiler_params=pltpu.CompilerParams(vmem_limit_bytes=48 * 2**20),
        cost_estimate=pl.CostEstimate(
            flops=8 * 10**9, bytes_accessed=2 * 10**7, transcendentals=2 * 10**6
        ),
        name="assign",
    )(flag, dest, more_dest, live, rows, more, panels)


def lookup_kernel(place_ref, table_ref, out_ref):
    slots, rows = table_ref.shape[1], place_ref.shape[1]
    table = table_ref[...]
    hi = table.astype(BF)
    rest = table - hi.astype(F32)
    mid = rest.astype(BF)
    low = (rest - mid.astype(F32)).astype(BF)
    hot = onehot(iota((slots, rows), 0) == place_ref[1:2, :])
    value = dot(hi, hot) + dot(mid, hot) + dot(low, hot)
    mine = iota(value.shape, 0) == place_ref[2:3, :]
    out_ref[...] = jnp.sum(jnp.where(mine, value, 0.0), axis=0, keepdims=True)


def lookup(place, table):
    return pl.pallas_call(
        lookup_kernel,
        out_shape=jax.ShapeDtypeStruct((1, place.shape[1]), F32),
        cost_estimate=pl.CostEstimate(flops=10**8, bytes_accessed=10**5, transcendentals=0),
        name="lookup",
    )(place, table)


def exchange(x, axes):
    return lax.all_to_all(x, axes, split_axis=0, concat_axis=0, tiled=True)


def local(points, coarse_id, owner_map, centroids):
    zn, cores = lax.axis_size("z"), lax.axis_size("core")
    dpn = lax.axis_size("y") * lax.axis_size("x")
    peers = dpn * cores
    bound = zn * CAP
    rows, width = points.shape
    per, rest = ROWS, bound - ROWS

    panel = exchange(centroids, ("y", "x")).reshape(-1, width)
    place, counts = index(coarse_id.reshape(1, rows), owner_map.reshape(1, -1), zn, dpn, cores, bound)
    packed = pack(place, points, peers, per, 0, bound).reshape(peers, per, width)
    arrived = exchange(packed, PLANE)
    panels = lax.all_gather(panel, "z", axis=0)

    mine = counts[0].reshape(peers, zn)
    most = jnp.max(jnp.sum(mine, axis=1))
    most = jnp.max(exchange(jnp.broadcast_to(most, (zn, 128)), "z"))
    sent = jnp.concatenate([mine, jnp.broadcast_to(most, (peers, zn))], axis=1)
    got = exchange(sent, PLANE)
    over = jnp.max(got[:, zn]) > per
    got = got[:, :zn]
    ends = jnp.cumsum(got, axis=1)
    at = jnp.arange(bound, dtype=jnp.int32)[None, :, None]
    slot_at = jnp.sum((at >= ends[:, None, :]).astype(jnp.int32), axis=2)
    begin = jnp.sum(jnp.where(at >= ends[:, None, :], got[:, None, :], 0), axis=2)
    side = (jnp.arange(peers, dtype=jnp.int32) % 2)[:, None]
    dest = slot_at * (2 * CAP) + side * CAP + at[:, :, 0] - begin
    dest = jnp.where(slot_at < zn, dest, -1)
    live = jnp.arange(CAP, dtype=jnp.int32)[None, None, :] < got.T[:, :, None]
    live = live.astype(F32).reshape(zn, peers * CAP)

    more = lax.cond(
        over,
        lambda: exchange(
            pack(place, points, peers, rest, per, bound).reshape(peers, rest, width), PLANE
        ).reshape(peers * rest, width),
        lambda: jnp.zeros((peers * rest, width), BF),
    )
    sums, mass, score = assign(
        over.astype(jnp.int32).reshape(1),
        dest[:, :per].reshape(peers // 2, 2 * per),
        dest[:, per:].reshape(peers // 2, 2 * rest),
        live,
        arrived.reshape(peers * per, width),
        more,
        panels,
    )
    sums = lax.psum_scatter(sums, "z", scatter_dimension=0, tiled=True)[0]
    score = score.reshape(zn, peers, CAP).transpose(1, 0, 2).reshape(peers, zn * CAP)
    score = exchange(score, PLANE).reshape(peers * zn, CAP).T
    point_score = lookup(place, score).reshape(rows)
    mass = jnp.sum(exchange(mass, "z"), axis=0)
    updated = (sums.astype(F32) + PRIOR * panel.astype(F32)) / (mass[:, None] + PRIOR)
    updated = updated.astype(BF).reshape(dpn, -1, width)
    return exchange(updated, ("y", "x")), point_score


def solution(mesh):
    devices = mesh.devices
    chips = Mesh(devices.reshape(4, 4, 8, 2), ("y", "x", "z", "core"))
    every = ("y", "x", "z", "core")
    grid = P(("z", "core"), ("y", "x"), None)
    return jax.shard_map(
        local,
        mesh=chips,
        in_specs=(P(every, None), P(every, None), P(), grid),
        out_specs=(grid, P(every)),
        check_vma=False,
    )
```

time: 408 us -> 242 us (0.59); the launches traced: 403 us -> 241 us
  waiting for transfers between devices: 202 us -> 115 us
  blocking collectives: 70.8 us -> 16 us
  local copies, waits for them, and re-layouts: 56.1 us -> 8.9 us
  Pallas kernels: 0 us -> 44.3 us
  matrix products: 20.9 us -> 0 us
  starting transfers between devices: 20.7 us -> 37 us
  other arithmetic: 17.3 us -> 4.59 us
    all_to_all x3 -> x6, waiting for transfers between devices: 132 us -> 49 us  [exchange(): return lax.all_to_all(x, axes, split_axis=0, concat_axis=0, tiled=True)]
    unnamed x1 -> x0, blocking collectives: 70.8 us -> none
    pallas_call x0 -> x4, Pallas kernels: none -> 44.3 us  [the longest x1 21.2 us: assign(): pl.pallas_call(functools.partial(assign_kernel, pairs, zn), grid_spec=plt...]
    scatter x2 -> x0, local copies, waits for them, and re-layouts: 30.3 us -> none  [the longest x1 15.7 us: local(): jnp.zeros((total_slots * capacity, feature_width), jnp.bfloat16)]
    all_gather x1, waiting for transfers between devices: 69.7 us -> 42.5 us  [local(): panels = lax.all_gather(panel, 'z', axis=0)]
    reduce_scatter x1, waiting for transfers between devices: 0.09 us -> 23.2 us  [local(): sums = lax.psum_scatter(sums, 'z', scatter_dimension=0, tiled=True)[0]]
    dot_general x2 -> x0, matrix products: 20.9 us -> none  [the longest x1 10.8 us: local(): jnp.einsum('sjcd,jfd->sjcf', arrived, panels, preferred_element_type=jnp....]
    gather x1 -> x0, local copies, waits for them, and re-layouts: 20.5 us -> none  [local(): point_score = returned[placement]]
  transfers between devices with their start and end apart: 5 -> 8, of which waited for: 3 -> 6; matrix products, arithmetic and copies ran while one was open for 10% -> 2% of each run, Pallas kernels for 0% -> 9%
where the time goes in v1:
time: 242 us; the launch traced here: 241 us
  waiting for transfers between devices  115 us (48%)
  Pallas kernels  44.3 us (18%)
  starting transfers between devices  37 us (15%)
  blocking collectives  16 us (7%)
  between operations  14.9 us (6%)
  local copies, waits for them, and re-layouts  8.9 us (4%)
  other arithmetic  4.59 us (2%)
    all_to_all x6, waiting for transfers between devices, exchange(): return lax.all_to_all(x, axes, split_axis=0, concat_axis=0, tiled=True)  49 us
    all_gather x1, waiting for transfers between devices, local(): panels = lax.all_gather(panel, 'z', axis=0)  42.5 us
    all_to_all x6, starting transfers between devices, exchange(): return lax.all_to_all(x, axes, split_axis=0, concat_axis=0, tiled=True)  36.9 us
    reduce_scatter x1, waiting for transfers between devices, local(): sums = lax.psum_scatter(sums, 'z', scatter_dimension=0, tiled=True)[0]  23.2 us
    pallas_call x1, Pallas kernels, assign(): pl.pallas_call(functools.partial(assign_kernel, pairs, zn), grid_spec=plt...  21.2 us
    pallas_call x1, Pallas kernels, pack(): pl.pallas_call(functools.partial(pack_kernel, per, first, bound), grid=(p...  18.6 us
    all_to_all x1, blocking collectives, exchange(): return lax.all_to_all(x, axes, split_axis=0, concat_axis=0, tiled=True)  16 us
  transfers between devices with their start and end apart: 8, of which 6 were waited for; matrix products, arithmetic and copies ran while one was open for 2% of the time, Pallas kernels for 9%

profile of v1, /device:TPU:2, one launch (start us, length us, event | category | flops | bytes accessed | tf_op | source)
XLA Modules:
  0.0 241.0 jit_solution(5088847445375585988)
XLA Ops:
  7.2 2.4 %place.1 = (s32[8,2048]{1,0:T(8,128)S(1)}, s32[8,256]{1,0:T(8,128)}) custom-call(s32[1,2048]{1,0:T(1,128)} %bitcast.32, s32[1,256]{1,0:T(1,128)} %bitcast.33), custom_call_target="tpu_custom_call" | custom-call | flops 1000000000 | bytes 100000 | tf_op jit(solution)/shard_map/place/pallas_call | solution.py:67
  9.6 0.7 slice_reduce_fusion.1
  10.3 0.1 reshape_squeeze.3
  10.4 0.1 reduce_sum.36
  10.5 0.6 reduce_max.27
  11.2 0.6 broadcast_in_dim.18
  11.8 16.0 %all_to_all.57 = s32[8,1,128]{2,1,0:T(1,128)S(1)} all-to-all(s32[8,1,128]{2,1,0:T(1,128)S(1)} %broadcast_in_dim.18), channel_id=1, replica_groups=mesh['y'=4,'x'=4,'z'=8,'core'=2] {'z'}, dimensions={0} | all-to-all | bytes 8192 | tf_op jit(solution)/shard_map/all_to_all | solution.py:218
  27.8 0.6 reduce_max.28
  28.4 1.3 concatenate.3
  29.7 7.6 %all-to-all-start.2 = ((s32[32,1,16]{2,1,0:T(1,128)}), s32[32,1,16]{2,1,0:T(1,128)S(1)}, u32[]{:S(2)}, u32[]{:S(2)}) async-start(s32[32,1,16]{2,1,0:T(1,128)} %bitcast.6), calls=%async_computation.2 | async-start | bytes 32768 | tf_op jit(solution)/shard_map/all_to_all | solution.py:218
  37.3 6.1 %all-to-all-done.2 = s32[32,1,16]{2,1,0:T(1,128)S(1)} async-done(((s32[32,1,16]{2,1,0:T(1,128)}), s32[32,1,16]{2,1,0:T(1,128)S(1)}, u32[]{:S(2)}, u32[]{:S(2)}) %all-to-all-start.2) | async-done | bytes 2080 | tf_op jit(solution)/shard_map/all_to_all | solution.py:218
  43.4 0.7 slice_reduce_fusion
  44.8 0.2 conditional.1
  44.8 0.2 broadcast.44
  45.0 0.0 copy-start.2
  45.0 1.7 copy-done.2
  46.7 4.8 %all-to-all-start.4 = ((bf16[16,16,768]{2,1,0:T(8,128)(2,1)}), bf16[16,16,768]{2,1,0:T(8,128)(2,1)S(1)}, u32[]{:S(2)}, u32[]{:S(2)}) async-start(bf16[16,16,768]{2,1,0:T(8,128)(2,1)} %param.9), calls=%async_computation.4 | async-start | bytes 786432 | tf_op jit(solution)/shard_map/all_to_all | solution.py:218
  51.4 18.6 %pack.3 = bf16[4096,768]{1,0:T(8,128)(2,1)} custom-call(s32[8,2048]{1,0:T(8,128)S(1)} %get-tuple-element.17.place_ref, bf16[2048,768]{1,0:T(8,128)(2,1)} %points_ref.1), custom_call_target="tpu_custom_call" | custom-call | flops 12884901888 | bytes 10000000 | tf_op jit(solution)/shard_map/pack/pallas_call | solution.py:91
  70.1 0.0 all-to-all-done.4
  70.1 0.0 copy-start
  70.1 0.7 copy-done
  70.8 7.5 %all-to-all-start.3 = ((bf16[32,128,768]{2,1,0:T(8,128)(2,1)}), bf16[32,128,768]{2,1,0:T(8,128)(2,1)}, u32[]{:S(2)}, u32[]{:S(2)}) async-start(bf16[32,128,768]{2,1,0:T(8,128)(2,1)} %bitcast.22), calls=%async_computation.3 | async-start | bytes 12582912 | tf_op jit(solution)/shard_map/all_to_all | solution.py:218
  78.3 0.0 all-gather.2.cloned.1.call-start
  78.3 0.7 all-gather.2.cloned.1.call-update
  79.0 0.0 reduce-scatter.2.cloned.1.call-start
  79.1 0.1 lt.36
  79.2 0.2 reduce_window_sum.11
  79.4 0.2 convert_reduce_fusion
  79.6 0.1 subtract_select_fusion
  79.7 0.1 reshape.91.more_dest_ref
  79.8 0.1 copy.24
  79.9 0.1 lt.38
  80.0 0.1 lt.39
  80.1 42.5 %all-gather.2.cloned.1.call-done.panel_ref = bf16[8,256,768]{2,1,0:T(8,128)(2,1)} async-done(((bf16[1,256,768]{2,1,0:T(8,128)(2,1)}), bf16[8,256,768]{2,1,0:T(8,128)(2,1)}) %all-gather.2.cloned.1.call-update) | async-done | bytes 3145744 | tf_op jit(solution)/shard_map/all_gather | solution.py:233
  122.6 30.9 %all-to-all-done.3 = bf16[32,128,768]{2,1,0:T(8,128)(2,1)} async-done(((bf16[32,128,768]{2,1,0:T(8,128)(2,1)}), bf16[32,128,768]{2,1,0:T(8,128)(2,1)}, u32[]{:S(2)}, u32[]{:S(2)}) %all-to-all-start.3) | async-done | bytes 6291488 | tf_op jit(solution)/shard_map/all_to_all | solution.py:218
  153.5 21.2 %assign.1 = (bf16[8,256,768]{2,1,0:T(8,128)(2,1)}, f32[8,256]{1,0:T(8,128)S(1)}, f32[8,768]{1,0:T(8,128)S(1)}) custom-call(s32[1]{0:T(128)} %bitcast.8.flag_ref, s32[16,256]{1,0:T(8,128)S(1)} %reshape.90.dest_ref, s32[16,128]{1,0:T(8,128)S(1)} %reshape.91.more_dest_ref, f32[8,768]{1,0:T(8,128)S(1)} %compare_convert_fusion.live_ref, ...), custom_call_target="tpu_custom_call" | custom-call | flops 8000000000 | bytes 20000000 | tf_op jit(solution)/shard_map/assign/pallas_call | solution.py:159
  174.7 0.0 copy-start.1
  174.7 0.0 reduce-scatter.2.cloned.1.call-update
  174.7 0.6 copy.25
  175.3 3.3 %all-to-all-start.5 = ((f32[8,1,256]{2,1,0:T(1,128)}), f32[8,1,256]{2,1,0:T(1,128)S(1)}, u32[]{:S(2)}, u32[]{:S(2)}) async-start(f32[8,1,256]{2,1,0:T(1,128)} %copy.25), calls=%async_computation.6 | async-start | bytes 16384 | tf_op jit(solution)/shard_map/all_to_all | solution.py:218
  178.6 0.1 reshape.94
  178.8 0.1 copy.26
  178.8 0.7 all_to_all.47
  179.6 6.9 %all-to-all-done.5 = f32[8,1,256]{2,1,0:T(1,128)S(1)} async-done(((f32[8,1,256]{2,1,0:T(1,128)}), f32[8,1,256]{2,1,0:T(1,128)S(1)}, u32[]{:S(2)}, u32[]{:S(2)}) %all-to-all-start.5) | async-done | bytes 8224 | tf_op jit(solution)/shard_map/all_to_all | solution.py:218
  186.5 6.6 %all-to-all-start.7 = ((f32[32,1,192]{2,1,0:T(1,128)}), f32[32,1,192]{2,1,0:T(1,128)S(1)}, u32[]{:S(2)}, u32[]{:S(2)}) async-start(f32[32,1,192]{2,1,0:T(1,128)} %all_to_all.47), calls=%async_computation.8 | async-start | bytes 65536 | tf_op jit(solution)/shard_map/all_to_all | solution.py:218
  193.1 0.1 add.56
  193.2 23.2 %reduce-scatter.2.cloned.1.call-done = bf16[1,256,768]{2,1,0:T(8,128)(2,1)} async-done(((bf16[8,256,768]{2,1,0:T(8,128)(2,1)}), bf16[1,256,768]{2,1,0:T(8,128)(2,1)}) %reduce-scatter.2.cloned.1.call-update) | async-done | bytes 393232 | tf_op jit(solution)/shard_map/reduce_scatter | solution.py:268
  216.3 0.0 copy-done.1
  216.3 1.9 fusion.1
  218.2 0.0 all-to-all-done.7
  218.2 7.2 %all-to-all-start.6 = ((bf16[16,16,768]{2,1,0:T(8,128)(2,1)}), bf16[16,16,768]{2,1,0:T(8,128)(2,1)S(1)}, u32[]{:S(2)}, u32[]{:S(2)}) async-start(bf16[16,16,768]{2,1,0:T(8,128)(2,1)} %fusion.1), calls=%async_computation.7 | async-start | bytes 786432 | tf_op jit(solution)/shard_map/all_to_all | solution.py:218
  225.4 0.1 reduce.4
  225.5 0.1 reshape.95
  225.6 0.7 copy.28
  226.3 2.1 lookup.1
  228.3 5.1 %all-to-all-done.6 = bf16[16,16,768]{2,1,0:T(8,128)(2,1)S(1)} async-done(((bf16[16,16,768]{2,1,0:T(8,128)(2,1)}), bf16[16,16,768]{2,1,0:T(8,128)(2,1)S(1)}, u32[]{:S(2)}, u32[]{:S(2)}) %all-to-all-start.6) | async-done | bytes 393248 | tf_op jit(solution)/shard_map/all_to_all | solution.py:218
  233.4 0.7 copy.32
  (9 shorter events, 0.1 us)
Async XLA Ops:
  29.7 13.7 %all-to-all-start.2 = ((s32[32,1,16]{2,1,0:T(1,128)}), s32[32,1,16]{2,1,0:T(1,128)S(1)}, u32[]{:S(2)}, u32[]{:S(2)}) async-start(s32[32,1,16]{2,1,0:T(1,128)} %bitcast.6), calls=%async_computation.2 | async-start | bytes 32768 | tf_op jit(solution)/shard_map/all_to_all | solution.py:218
  45.0 1.7 copy-start.2
  46.7 23.4 %all-to-all-start.4 = ((bf16[16,16,768]{2,1,0:T(8,128)(2,1)}), bf16[16,16,768]{2,1,0:T(8,128)(2,1)S(1)}, u32[]{:S(2)}, u32[]{:S(2)}) async-start(bf16[16,16,768]{2,1,0:T(8,128)(2,1)} %param.9), calls=%async_computation.4 | async-start | bytes 786432 | tf_op jit(solution)/shard_map/all_to_all | solution.py:218
  70.1 0.7 copy-start
  70.8 82.7 %all-to-all-start.3 = ((bf16[32,128,768]{2,1,0:T(8,128)(2,1)}), bf16[32,128,768]{2,1,0:T(8,128)(2,1)}, u32[]{:S(2)}, u32[]{:S(2)}) async-start(bf16[32,128,768]{2,1,0:T(8,128)(2,1)} %bitcast.22), calls=%async_computation.3 | async-start | bytes 12582912 | tf_op jit(solution)/shard_map/all_to_all | solution.py:218
  78.3 44.3 %all-gather.2.cloned.1.call-start = ((), (), s32[]{:S(2)}) async-start(), calls=%async_computation.9 | async-start | bytes 3538944 | tf_op jit(solution)/shard_map/all_gather | solution.py:233
  79.0 137.3 %reduce-scatter.2.cloned.1.call-start = ((), (), s32[]{:S(2)}) async-start(), calls=%async_computation.10 | async-start | bytes 3538944 | tf_op jit(solution)/shard_map/reduce_scatter | solution.py:268
  174.7 41.7 %copy-start.1 = (bf16[16,16,768]{2,1,0:T(8,128)(2,1)S(1)}, bf16[16,16,768]{2,1,0:T(8,128)(2,1)}, u32[]{:S(2)}) copy-start(bf16[16,16,768]{2,1,0:T(8,128)(2,1)} %copy-done) | copy-start | bytes 1179652
  175.3 11.2 %all-to-all-start.5 = ((f32[8,1,256]{2,1,0:T(1,128)}), f32[8,1,256]{2,1,0:T(1,128)S(1)}, u32[]{:S(2)}, u32[]{:S(2)}) async-start(f32[8,1,256]{2,1,0:T(1,128)} %copy.25), calls=%async_computation.6 | async-start | bytes 16384 | tf_op jit(solution)/shard_map/all_to_all | solution.py:218
  186.5 31.8 %all-to-all-start.7 = ((f32[32,1,192]{2,1,0:T(1,128)}), f32[32,1,192]{2,1,0:T(1,128)S(1)}, u32[]{:S(2)}, u32[]{:S(2)}) async-start(f32[32,1,192]{2,1,0:T(1,128)} %all_to_all.47), calls=%async_computation.8 | async-start | bytes 65536 | tf_op jit(solution)/shard_map/all_to_all | solution.py:218
  218.2 15.2 %all-to-all-start.6 = ((bf16[16,16,768]{2,1,0:T(8,128)(2,1)}), bf16[16,16,768]{2,1,0:T(8,128)(2,1)S(1)}, u32[]{:S(2)}, u32[]{:S(2)}) async-start(bf16[16,16,768]{2,1,0:T(8,128)(2,1)} %fusion.1), calls=%async_computation.7 | async-start | bytes 786432 | tf_op jit(solution)/shard_map/all_to_all | solution.py:218
Sparse Core Ops, SparseCore 0:
  81.5 41.0 all-gather.1
  174.8 41.4 reduce-scatter.1

commit v2 on v1

v2 whole, which is shorter than its diff:
```python
import functools
import jax
import jax.numpy as jnp
from jax import lax
from jax.experimental import pallas as pl
from jax.experimental.pallas import tpu as pltpu
from jax.sharding import Mesh, PartitionSpec as P

PRIOR = 4.0
CAP = 24
ROWS = 128
SOME, REST = 16, 72
PLANE = ("y", "x", "core")
BF = jnp.bfloat16
F32 = jnp.float32


def iota(shape, dim):
    return lax.broadcasted_iota(jnp.int32, shape, dim)


def dot(a, b, dims=((1,), (0,))):
    return lax.dot_general(a, b, (dims, ((), ())), preferred_element_type=F32)


def onehot(mask):
    return jnp.where(mask, 1.0, 0.0).astype(BF)


def index_kernel(zn, dpn, cores, bound, coarse_ref, owner_ref, place_ref, note_ref, hot_ref):
    slots = owner_ref.shape[1]
    rows = coarse_ref.shape[1]
    peers, width = note_ref.shape
    owner = owner_ref[...]
    column, cluster = owner % dpn, owner // dpn
    lane_of = (column * cores + cluster % cores) * zn + cluster // cores
    move = onehot(iota((slots, slots), 0) == lane_of)
    blk = 256
    earlier = onehot(iota((blk, blk), 0) < iota((blk, blk), 1))
    carry = jnp.zeros((slots, 1), F32)
    ranks = []
    for b in range(rows // blk):
        named = onehot(iota((slots, blk), 0) == coarse_ref[:, b * blk : (b + 1) * blk])
        hot = dot(move, named)
        hot_bf = hot.astype(BF)
        hot_ref[:, b * blk : (b + 1) * blk] = hot_bf
        before = dot(hot_bf, earlier) + carry
        ranks.append(jnp.sum(hot * before, axis=0, keepdims=True))
        carry = carry + jnp.sum(hot, axis=1, keepdims=True)
    rank = jnp.concatenate(ranks, axis=1)
    hot_all = hot_ref[...]
    counts = dot(jnp.ones((8, rows), BF), hot_all, ((1,), (1,)))
    la, lb = iota((slots, slots), 0), iota((slots, slots), 1)
    group = onehot((la // zn == lb // zn) & (la < lb))
    offset = dot(counts.astype(BF), group)
    which = iota((8, slots), 0)
    query = jnp.where(which == 0, offset, iota((8, slots), 1).astype(F32)).astype(BF)
    found = dot(query, hot_all)
    lane = found[1:2].astype(jnp.int32)
    rank = rank.astype(jnp.int32)
    pos = (lane // zn) * bound + found[0:1].astype(jnp.int32) + rank
    row = iota((8, rows), 0)
    place_ref[...] = jnp.where(row == 0, pos, jnp.where(row == 1, lane, rank))
    mine = iota((peers, slots), 1) // zn == iota((peers, slots), 0)
    spread = jnp.where(mine, counts[0:1], 0.0)
    most = jnp.max(jnp.sum(spread, axis=1, keepdims=True), axis=0, keepdims=True)
    spot = onehot(iota((slots, width), 0) % zn == iota((slots, width), 1))
    note = dot(spread.astype(BF), spot)
    note_ref[...] = jnp.where(iota((peers, width), 1) == zn, most, note).astype(BF)


def index(coarse, owner, zn, dpn, cores, bound, width):
    rows, slots = coarse.shape[1], owner.shape[1]
    return pl.pallas_call(
        functools.partial(index_kernel, zn, dpn, cores, bound),
        out_shape=(
            jax.ShapeDtypeStruct((8, rows), jnp.int32),
            jax.ShapeDtypeStruct((dpn * cores, width), BF),
        ),
        scratch_shapes=[pltpu.VMEM((slots, rows), BF)],
        cost_estimate=pl.CostEstimate(flops=10**9, bytes_accessed=10**5, transcendentals=0),
        name="place",
    )(coarse, owner)


def pack_kernel(per, first, bound, noted, place_ref, points_ref, note_ref, out_ref):
    g = pl.program_id(0)
    tall = out_ref.shape[0]
    i = iota((tall, 1), 0)
    peer, at = g * (tall // per) + i // per, i % per
    want = peer * bound + first + at
    if noted:
        want = jnp.where(at == per - 1, -1, want)
    pick = onehot(place_ref[0:1, :] == want)
    packed = dot(pick, points_ref[...])
    if noted:
        peers = note_ref.shape[0]
        which = jnp.where(at == per - 1, peer, -1)
        packed = packed + dot(onehot(iota((tall, peers), 1) == which), note_ref[...])
    out_ref[...] = packed.astype(BF)


def pack(place, points, note, per, first, bound, tall, noted):
    rows, width = points.shape
    peers = note.shape[0]
    return pl.pallas_call(
        functools.partial(pack_kernel, per, first, bound, noted),
        grid=(peers * per // tall,),
        in_specs=[
            pl.BlockSpec((8, rows), lambda g: (0, 0)),
            pl.BlockSpec((rows, width), lambda g: (0, 0)),
            pl.BlockSpec((peers, width), lambda g: (0, 0)),
        ],
        out_specs=pl.BlockSpec((tall, width), lambda g: (g, 0)),
        out_shape=jax.ShapeDtypeStruct((peers * per, width), BF),
        cost_estimate=pl.CostEstimate(
            flops=2 * peers * per * rows * width, bytes_accessed=10**7, transcendentals=0
        ),
        name="pack",
    )(place, points, note)


def places(zn, notes, per, first, count):
    lane, sub = iota((zn, 128), 1), iota((zn, 128), 0)
    sides = []
    for note in notes:
        note = jnp.broadcast_to(note, (zn, 128))
        ends = jnp.sum(jnp.where(lane <= sub, note, 0.0), axis=1, keepdims=True)
        size = jnp.sum(jnp.where(lane == sub, note, 0.0), axis=1, keepdims=True)
        sides.append((ends, size))
    c = iota((zn, 2 * per), 1)
    second = c >= per
    at = c - jnp.where(second, per, 0)
    pos = (at + first).astype(F32)
    passed = pos >= jnp.where(second, sides[1][0], sides[0][0])
    size = jnp.where(second, sides[1][1], sides[0][1])
    slot = jnp.sum(jnp.where(passed, 1.0, 0.0), axis=0, keepdims=True)
    begin = jnp.sum(jnp.where(passed, size, 0.0), axis=0, keepdims=True)
    side = jnp.where(second[0:1], 1.0 * CAP, 0.0)
    dest = slot * (2 * CAP) + side + pos[0:1] - begin
    return jnp.where(at[0:1] < count, dest, -1.0).astype(jnp.int32)


def assign_kernel(
    pairs, zn, flag_ref, in_ref, more_ref, panel_ref, sums_ref, mass_ref, score_ref, held, more_vmem
):
    g = pl.program_id(0)
    pad = 2 * CAP
    tall = zn * pad
    width = in_ref.shape[1]
    per, rest = in_ref.shape[0] // 2, more_vmem.shape[0] // 2
    top = zn // 2

    @pl.when(g < pairs)
    def _():
        notes = [in_ref[k * per - 1 : k * per, 0:128].astype(F32) for k in (1, 2)]
        start = pl.multiple_of(g * pad, 16)

        def lay(block, dest, add):
            pick = jnp.where(iota((tall, block.shape[0]), 0) == dest, 1.0, 0.0)
            there = jnp.broadcast_to(jnp.sum(pick, axis=1, keepdims=True), (tall, 128))
            laid = dot(pick.astype(BF), block)
            for j in range(zn):
                part = slice(j * pad, (j + 1) * pad)
                for value, lanes in ((laid[part], slice(0, width)), (there[part], slice(width, width + 128))):
                    if add:
                        value = value + held[j, pl.ds(start, pad), lanes].astype(F32)
                    held[j, pl.ds(start, pad), lanes] = value.astype(BF)

        lay(in_ref[...], places(zn, notes, per, 0, per - 1), False)

        @pl.when(flag_ref[0] != 0)
        def _():
            deep = 2 * rest
            pltpu.sync_copy(more_ref.at[pl.ds(pl.multiple_of(g * deep, 16), deep), :], more_vmem)
            lay(more_vmem[...], places(zn, notes, rest, per - 1, rest), True)

    @pl.when(g >= pairs)
    def _():
        j = g - pairs
        x = held[j]
        panel = panel_ref[0]
        wide = panel.astype(F32)
        sqnorm = jnp.sum(wide * wide, axis=1, keepdims=True)
        logits = dot(panel, x[:, :width], ((1,), (1,))) - 0.5 * sqnorm
        peak = jnp.max(logits, axis=0, keepdims=True)
        shifted = jnp.exp(logits - peak)
        total = jnp.sum(shifted, axis=0, keepdims=True)
        score_ref[pl.ds(j, 1), :] = peak + jnp.log(total)
        weights = (shifted * (1.0 / total)).astype(BF)
        sums = dot(weights, x)
        sums_ref[0] = sums[:, :width].astype(BF)
        mass_ref[pl.ds(j, 1), :] = jnp.transpose(sums[:, width:])[0:1]


def assign(flag, rows, more, panels, pairs):
    zn, fine, width = panels.shape
    deep, more_deep = rows.shape[0] // pairs, more.shape[0] // pairs
    spread = pairs * 2 * CAP
    last = pairs - 1
    whole = lambda g, f: (0, 0)
    return pl.pallas_call(
        functools.partial(assign_kernel, pairs, zn),
        grid_spec=pltpu.PrefetchScalarGridSpec(
            num_scalar_prefetch=1,
            grid=(pairs + zn,),
            in_specs=[
                pl.BlockSpec((deep, width), lambda g, f: (jnp.minimum(g, last), 0)),
                pl.BlockSpec(memory_space=pl.ANY),
                pl.BlockSpec((1, fine, width), lambda g, f: (jnp.maximum(g - pairs, 0), 0, 0)),
            ],
            out_specs=[
                pl.BlockSpec((1, fine, width), lambda g, f: (jnp.maximum(g - pairs, 0), 0, 0)),
                pl.BlockSpec((zn, fine), whole),
                pl.BlockSpec((zn, spread), whole),
            ],
            scratch_shapes=[
                pltpu.VMEM((zn, spread, width + 128), BF),
                pltpu.VMEM((more_deep, width), BF),
            ],
        ),
        out_shape=(
            jax.ShapeDtypeStruct((zn, fine, width), BF),
            jax.ShapeDtypeStruct((zn, fine), F32),
            jax.ShapeDtypeStruct((zn, spread), F32),
        ),
        cost_estimate=pl.CostEstimate(
            flops=8 * 10**9, bytes_accessed=2 * 10**7, transcendentals=2 * 10**6
        ),
        name="assign",
    )(flag, rows, more, panels)


def lookup_kernel(place_ref, table_ref, out_ref):
    slots, rows = table_ref.shape[1], place_ref.shape[1]
    table = table_ref[...]
    hi = table.astype(BF)
    rest = table - hi.astype(F32)
    mid = rest.astype(BF)
    low = (rest - mid.astype(F32)).astype(BF)
    hot = onehot(iota((slots, rows), 0) == place_ref[1:2, :])
    value = dot(hi, hot) + dot(mid, hot) + dot(low, hot)
    mine = iota(value.shape, 0) == place_ref[2:3, :]
    out_ref[...] = jnp.sum(jnp.where(mine, value, 0.0), axis=0, keepdims=True)


def lookup(place, table):
    return pl.pallas_call(
        lookup_kernel,
        out_shape=jax.ShapeDtypeStruct((1, place.shape[1]), F32),
        cost_estimate=pl.CostEstimate(flops=10**8, bytes_accessed=10**5, transcendentals=0),
        name="lookup",
    )(place, table)


def exchange(x, axes):
    return lax.all_to_all(x, axes, split_axis=0, concat_axis=0, tiled=True)


def local(points, coarse_id, owner_map, centroids):
    zn, cores = lax.axis_size("z"), lax.axis_size("core")
    dpn = lax.axis_size("y") * lax.axis_size("x")
    peers = dpn * cores
    bound = zn * CAP
    rows, width = points.shape

    panel = exchange(centroids, ("y", "x")).reshape(-1, width)
    place, note = index(
        coarse_id.reshape(1, rows), owner_map.reshape(1, -1), zn, dpn, cores, bound, width
    )
    packed = pack(place, points, note, ROWS, 0, bound, 1024, True)
    arrived = exchange(packed.reshape(peers, ROWS, width), PLANE)
    panels = lax.all_gather(panel, "z", axis=0)

    most = jnp.max(arrived[:, ROWS - 1, zn].astype(F32))

    def second(per):
        block = pack(place, points, note, per, ROWS - 1, bound, 16 * per, False)
        block = exchange(block.reshape(peers, per, width), PLANE)
        return jnp.pad(block, ((0, 0), (0, REST - per), (0, 0))).reshape(peers * REST, width)

    level = (most > ROWS - 1).astype(jnp.int32) + (most > ROWS - 1 + SOME).astype(jnp.int32)
    more = lax.switch(
        level,
        (lambda: jnp.zeros((peers * REST, width), BF), lambda: second(SOME), lambda: second(REST)),
    )
    sums, mass, score = assign(
        level.reshape(1), arrived.reshape(peers * ROWS, width), more, panels, peers // 2
    )
    sums = lax.psum_scatter(sums, "z", scatter_dimension=0, tiled=True)[0]
    score = score.reshape(zn, peers, CAP).transpose(1, 0, 2).reshape(peers, zn * CAP)
    score = exchange(score, PLANE).reshape(peers * zn, CAP).T
    point_score = lookup(place, score).reshape(rows)
    mass = jnp.sum(exchange(mass, "z"), axis=0)
    updated = (sums.astype(F32) + PRIOR * panel.astype(F32)) / (mass[:, None] + PRIOR)
    updated = updated.astype(BF).reshape(dpn, -1, width)
    return exchange(updated, ("y", "x")), point_score


def solution(mesh):
    devices = mesh.devices
    chips = Mesh(devices.reshape(4, 4, 8, 2), ("y", "x", "z", "core"))
    every = ("y", "x", "z", "core")
    grid = P(("z", "core"), ("y", "x"), None)
    return jax.shard_map(
        local,
        mesh=chips,
        in_specs=(P(every, None), P(every, None), P(), grid),
        out_specs=(grid, P(every)),
        check_vma=False,
    )
```

time: 242 us -> 219 us (0.905)
  blocking collectives: 16 us -> 0 us
  waiting for transfers between devices: 115 us -> 110 us
  local copies, waits for them, and re-layouts: 8.9 us -> 5.6 us
    all_gather x1, waiting for transfers between devices: 42.5 us -> 0.02 us  [local(): panels = lax.all_gather(panel, 'z', axis=0)]
    all_to_all x6 -> x5, waiting for transfers between devices: 49 us -> 85.7 us  [exchange(): return lax.all_to_all(x, axes, split_axis=0, concat_axis=0, tiled=True)]
    all_to_all x1 -> x0, blocking collectives: 16 us -> none  [exchange(): return lax.all_to_all(x, axes, split_axis=0, concat_axis=0, tiled=True)]
    all_to_all x6 -> x5, starting transfers between devices: 36.9 us -> 37.5 us  [exchange(): return lax.all_to_all(x, axes, split_axis=0, concat_axis=0, tiled=True)]
  transfers between devices with their start and end apart: 8 -> 7, of which waited for: 6 -> 4; matrix products, arithmetic and copies ran while one was open for 2% -> 3% of each run, Pallas kernels for 9% -> 10%
where the time goes in v2:
time: 219 us; the launch traced here: 218 us
  waiting for transfers between devices  110 us (50%)
  Pallas kernels  45.1 us (21%)
  starting transfers between devices  37.5 us (17%)
  between operations  15.4 us (7%)
  local copies, waits for them, and re-layouts  5.6 us (3%)
  other arithmetic  3.56 us (2%)
    all_to_all x5, waiting for transfers between devices, exchange(): return lax.all_to_all(x, axes, split_axis=0, concat_axis=0, tiled=True)  85.7 us
    all_to_all x5, starting transfers between devices, exchange(): return lax.all_to_all(x, axes, split_axis=0, concat_axis=0, tiled=True)  37.5 us
    reduce_scatter x1, waiting for transfers between devices, local(): sums = lax.psum_scatter(sums, 'z', scatter_dimension=0, tiled=True)[0]  24.1 us
    pallas_call x1, Pallas kernels, assign(): pl.pallas_call(functools.partial(assign_kernel, pairs, zn), grid_spec=plt...  22.8 us
    pallas_call x1, Pallas kernels, pack(): pl.pallas_call(functools.partial(pack_kernel, per, first, bound, noted),...  17.2 us
  transfers between devices with their start and end apart: 7, of which 4 were waited for; matrix products, arithmetic and copies ran while one was open for 3% of the time, Pallas kernels for 10%

profile of v2, /device:TPU:2, one launch (start us, length us, event | category | flops | bytes accessed | tf_op | source)
XLA Modules:
  0.0 217.7 jit_solution(4604908523860711922)
XLA Ops:
  7.2 0.0 copy-start.2
  7.2 7.8 %all-to-all-start.3 = ((bf16[16,16,768]{2,1,0:T(8,128)(2,1)}), bf16[16,16,768]{2,1,0:T(8,128)(2,1)S(1)}, u32[]{:S(2)}, u32[]{:S(2)}) async-start(bf16[16,16,768]{2,1,0:T(8,128)(2,1)} %param.10), calls=%async_computation.3 | async-start | bytes 786432 | tf_op jit(solution)/shard_map/all_to_all | solution.py:257
  14.9 3.0 %place.1 = (s32[8,2048]{1,0:T(8,128)}, bf16[32,768]{1,0:T(8,128)(2,1)}) custom-call(s32[1,2048]{1,0:T(1,128)} %bitcast.26, s32[1,256]{1,0:T(1,128)} %bitcast.27), custom_call_target="tpu_custom_call" | custom-call | flops 1000000000 | bytes 100000 | tf_op jit(solution)/shard_map/place/pallas_call | solution.py:74
  17.9 0.0 copy-done.2
  17.9 17.2 %pack.5 = bf16[4096,768]{1,0:T(8,128)(2,1)} custom-call(s32[8,2048]{1,0:T(8,128)} %get-tuple-element.29.place_ref, bf16[2048,768]{1,0:T(8,128)(2,1)S(1)} %copy-done.2, bf16[32,768]{1,0:T(8,128)(2,1)} %get-tuple-element.30.note_ref), custom_call_target="tpu_custom_call" | custom-call | flops 12884901888 | bytes 10000000 | tf_op jit(solution)/shard_map/pack/pallas_call | solution.py:106
  35.1 0.0 all-to-all-done.3
  35.1 0.0 copy-start
  35.1 0.7 copy-done
  35.9 7.4 %all-to-all-start.2 = ((bf16[32,128,768]{2,1,0:T(8,128)(2,1)}), bf16[32,128,768]{2,1,0:T(8,128)(2,1)}, u32[]{:S(2)}, u32[]{:S(2)}) async-start(bf16[32,128,768]{2,1,0:T(8,128)(2,1)} %bitcast.16), calls=%async_computation.2 | async-start | bytes 12582912 | tf_op jit(solution)/shard_map/all_to_all | solution.py:257
  43.3 0.0 all-gather.2.cloned.1.call-start
  43.4 0.7 all-gather.2.cloned.1.call-update
  44.1 0.0 reduce-scatter.2.cloned.1.call-start
  44.1 74.4 %all-to-all-done.2 = bf16[32,128,768]{2,1,0:T(8,128)(2,1)} async-done(((bf16[32,128,768]{2,1,0:T(8,128)(2,1)}), bf16[32,128,768]{2,1,0:T(8,128)(2,1)}, u32[]{:S(2)}, u32[]{:S(2)}) %all-to-all-start.2) | async-done | bytes 6291488 | tf_op jit(solution)/shard_map/all_to_all | solution.py:257
  118.5 1.6 slice_reduce_fusion
  121.4 0.2 conditional.1
  121.4 0.2 broadcast.12
  121.6 0.0 all-gather.2.cloned.1.call-done.panel_ref
  121.7 22.8 %assign.1 = (bf16[8,256,768]{2,1,0:T(8,128)(2,1)}, f32[8,256]{1,0:T(8,128)}, f32[8,768]{1,0:T(8,128)}) custom-call(s32[1]{0:T(128)} %bitcast.7.flag_ref, bf16[4096,768]{1,0:T(8,128)(2,1)} %bitcast.8.in_ref, bf16[2304,768]{1,0:T(8,128)(2,1)S(1)} %get-tuple-element.38.more_ref, bf16[8,256,768]{2,1,0:T(8,128)(2,1)} %all-gather.2.cloned.1.call-done.panel_ref), custom_call_target="tpu_custom_call" | custom-call | flops 8000000000 | bytes 20000000 | tf_op jit(solution)/shard_map/assign/pallas_call | solution.py:202
  144.5 0.0 copy-start.1
  144.5 0.0 copy-start.3
  144.5 0.0 reduce-scatter.2.cloned.1.call-update
  144.5 1.3 copy.8
  145.9 8.5 %all-to-all-start.4 = ((f32[8,1,256]{2,1,0:T(1,128)}), f32[8,1,256]{2,1,0:T(1,128)S(1)}, u32[]{:S(2)}, u32[]{:S(2)}) async-start(f32[8,1,256]{2,1,0:T(1,128)} %copy.8), calls=%async_computation.5 | async-start | bytes 16384 | tf_op jit(solution)/shard_map/all_to_all | solution.py:257
  154.3 0.8 reshape.69
  155.2 0.1 copy.9
  155.3 0.8 all_to_all.34
  156.0 6.1 %all-to-all-done.4 = f32[8,1,256]{2,1,0:T(1,128)S(1)} async-done(((f32[8,1,256]{2,1,0:T(1,128)}), f32[8,1,256]{2,1,0:T(1,128)S(1)}, u32[]{:S(2)}, u32[]{:S(2)}) %all-to-all-start.4) | async-done | bytes 8224 | tf_op jit(solution)/shard_map/all_to_all | solution.py:257
  162.1 6.5 %all-to-all-start.6 = ((f32[32,1,192]{2,1,0:T(1,128)}), f32[32,1,192]{2,1,0:T(1,128)S(1)}, u32[]{:S(2)}, u32[]{:S(2)}) async-start(f32[32,1,192]{2,1,0:T(1,128)} %all_to_all.34), calls=%async_computation.7 | async-start | bytes 65536 | tf_op jit(solution)/shard_map/all_to_all | solution.py:257
  168.7 0.1 add.29
  168.8 24.1 %reduce-scatter.2.cloned.1.call-done = bf16[1,256,768]{2,1,0:T(8,128)(2,1)} async-done(((bf16[8,256,768]{2,1,0:T(8,128)(2,1)}), bf16[1,256,768]{2,1,0:T(8,128)(2,1)}) %reduce-scatter.2.cloned.1.call-update) | async-done | bytes 393232 | tf_op jit(solution)/shard_map/reduce_scatter | solution.py:290
  192.8 0.0 copy-done.1
  192.9 1.9 fusion.1
  194.7 0.0 all-to-all-done.6
  194.7 7.3 %all-to-all-start.5 = ((bf16[16,16,768]{2,1,0:T(8,128)(2,1)}), bf16[16,16,768]{2,1,0:T(8,128)(2,1)S(1)}, u32[]{:S(2)}, u32[]{:S(2)}) async-start(bf16[16,16,768]{2,1,0:T(8,128)(2,1)} %fusion.1), calls=%async_computation.6 | async-start | bytes 786432 | tf_op jit(solution)/shard_map/all_to_all | solution.py:257
  202.0 0.1 reduce.3
  202.1 0.1 reshape.70
  202.2 0.7 copy.11
  202.9 0.0 copy-done.3
  202.9 2.1 lookup.1
  205.0 5.1 %all-to-all-done.5 = bf16[16,16,768]{2,1,0:T(8,128)(2,1)S(1)} async-done(((bf16[16,16,768]{2,1,0:T(8,128)(2,1)}), bf16[16,16,768]{2,1,0:T(8,128)(2,1)S(1)}, u32[]{:S(2)}, u32[]{:S(2)}) %all-to-all-start.5) | async-done | bytes 393248 | tf_op jit(solution)/shard_map/all_to_all | solution.py:257
  210.1 0.7 copy.16
  (2 shorter events, 0.0 us)
Async XLA Ops:
  7.2 10.7 %copy-start.2 = (bf16[2048,768]{1,0:T(8,128)(2,1)S(1)}, bf16[2048,768]{1,0:T(8,128)(2,1)}, u32[]{:S(2)}) copy-start(bf16[2048,768]{1,0:T(8,128)(2,1)} %points_ref.1) | copy-start | bytes 9437188
  7.2 28.0 %all-to-all-start.3 = ((bf16[16,16,768]{2,1,0:T(8,128)(2,1)}), bf16[16,16,768]{2,1,0:T(8,128)(2,1)S(1)}, u32[]{:S(2)}, u32[]{:S(2)}) async-start(bf16[16,16,768]{2,1,0:T(8,128)(2,1)} %param.10), calls=%async_computation.3 | async-start | bytes 786432 | tf_op jit(solution)/shard_map/all_to_all | solution.py:257
  35.1 0.7 copy-start
  35.9 82.6 %all-to-all-start.2 = ((bf16[32,128,768]{2,1,0:T(8,128)(2,1)}), bf16[32,128,768]{2,1,0:T(8,128)(2,1)}, u32[]{:S(2)}, u32[]{:S(2)}) async-start(bf16[32,128,768]{2,1,0:T(8,128)(2,1)} %bitcast.16), calls=%async_computation.2 | async-start | bytes 12582912 | tf_op jit(solution)/shard_map/all_to_all | solution.py:257
  43.3 78.3 %all-gather.2.cloned.1.call-start = ((), (), s32[]{:S(2)}) async-start(), calls=%async_computation.8 | async-start | bytes 3538944 | tf_op jit(solution)/shard_map/all_gather | solution.py:273
  44.1 148.8 %reduce-scatter.2.cloned.1.call-start = ((), (), s32[]{:S(2)}) async-start(), calls=%async_computation.9 | async-start | bytes 3538944 | tf_op jit(solution)/shard_map/reduce_scatter | solution.py:290
  144.5 48.3 %copy-start.1 = (bf16[16,16,768]{2,1,0:T(8,128)(2,1)S(1)}, bf16[16,16,768]{2,1,0:T(8,128)(2,1)}, u32[]{:S(2)}) copy-start(bf16[16,16,768]{2,1,0:T(8,128)(2,1)} %copy-done) | copy-start | bytes 1179652
  144.5 58.4 %copy-start.3 = (s32[8,2048]{1,0:T(8,128)S(1)}, s32[8,2048]{1,0:T(8,128)}, u32[]{:S(2)}) copy-start(s32[8,2048]{1,0:T(8,128)} %get-tuple-element.29.place_ref) | copy-start | bytes 196612
  145.9 16.3 %all-to-all-start.4 = ((f32[8,1,256]{2,1,0:T(1,128)}), f32[8,1,256]{2,1,0:T(1,128)S(1)}, u32[]{:S(2)}, u32[]{:S(2)}) async-start(f32[8,1,256]{2,1,0:T(1,128)} %copy.8), calls=%async_computation.5 | async-start | bytes 16384 | tf_op jit(solution)/shard_map/all_to_all | solution.py:257
  162.1 32.6 %all-to-all-start.6 = ((f32[32,1,192]{2,1,0:T(1,128)}), f32[32,1,192]{2,1,0:T(1,128)S(1)}, u32[]{:S(2)}, u32[]{:S(2)}) async-start(f32[32,1,192]{2,1,0:T(1,128)} %all_to_all.34), calls=%async_computation.7 | async-start | bytes 65536 | tf_op jit(solution)/shard_map/all_to_all | solution.py:257
  194.7 15.3 %all-to-all-start.5 = ((bf16[16,16,768]{2,1,0:T(8,128)(2,1)}), bf16[16,16,768]{2,1,0:T(8,128)(2,1)S(1)}, u32[]{:S(2)}, u32[]{:S(2)}) async-start(bf16[16,16,768]{2,1,0:T(8,128)(2,1)} %fusion.1), calls=%async_computation.6 | async-start | bytes 786432 | tf_op jit(solution)/shard_map/all_to_all | solution.py:257
Sparse Core Ops, SparseCore 0:
  46.5 47.6 all-gather.1
  144.7 48.1 reduce-scatter.1

commit v3 on v2

--- a/solution.py
+++ b/solution.py
@@ -66,16 +66,16 @@
     most = jnp.max(jnp.sum(spread, axis=1, keepdims=True), axis=0, keepdims=True)
     spot = onehot(iota((slots, width), 0) % zn == iota((slots, width), 1))
     note = dot(spread.astype(BF), spot)
-    note_ref[...] = jnp.where(iota((peers, width), 1) == zn, most, note).astype(BF)
-
-
-def index(coarse, owner, zn, dpn, cores, bound, width):
+    note_ref[...] = jnp.where(iota((peers, width), 1) == zn, most, note)
+
+
+def index(coarse, owner, zn, dpn, cores, bound):
     rows, slots = coarse.shape[1], owner.shape[1]
     return pl.pallas_call(
         functools.partial(index_kernel, zn, dpn, cores, bound),
         out_shape=(
             jax.ShapeDtypeStruct((8, rows), jnp.int32),
-            jax.ShapeDtypeStruct((dpn * cores, width), BF),
+            jax.ShapeDtypeStruct((dpn * cores, 128), F32),
         ),
         scratch_shapes=[pltpu.VMEM((slots, rows), BF)],
         cost_estimate=pl.CostEstimate(flops=10**9, bytes_accessed=10**5, transcendentals=0),
@@ -85,19 +85,19 @@
 
 def pack_kernel(per, first, bound, noted, place_ref, points_ref, note_ref, out_ref):
     g = pl.program_id(0)
-    tall = out_ref.shape[0]
+    tall, width = out_ref.shape
     i = iota((tall, 1), 0)
     peer, at = g * (tall // per) + i // per, i % per
     want = peer * bound + first + at
-    if noted:
-        want = jnp.where(at == per - 1, -1, want)
     pick = onehot(place_ref[0:1, :] == want)
     packed = dot(pick, points_ref[...])
+    out_ref[...] = packed.astype(BF)
     if noted:
-        peers = note_ref.shape[0]
-        which = jnp.where(at == per - 1, peer, -1)
-        packed = packed + dot(onehot(iota((tall, peers), 1) == which), note_ref[...])
-    out_ref[...] = packed.astype(BF)
+        for k in range(tall // per):
+            tile = slice((k + 1) * per - 16, (k + 1) * per)
+            note = jnp.broadcast_to(note_ref[k : k + 1], (16, 128))
+            end = iota((16, 128), 0) == 15
+            out_ref[tile, :128] = jnp.where(end, note, packed[tile, :128]).astype(BF)
 
 
 def pack(place, points, note, per, first, bound, tall, noted):
@@ -109,7 +109,7 @@
         in_specs=[
             pl.BlockSpec((8, rows), lambda g: (0, 0)),
             pl.BlockSpec((rows, width), lambda g: (0, 0)),
-            pl.BlockSpec((peers, width), lambda g: (0, 0)),
+            pl.BlockSpec((tall // per, 128), lambda g: (g, 0)),
         ],
         out_specs=pl.BlockSpec((tall, width), lambda g: (g, 0)),
         out_shape=jax.ShapeDtypeStruct((peers * per, width), BF),
@@ -142,75 +142,88 @@
 
 
 def assign_kernel(
-    pairs, zn, flag_ref, in_ref, more_ref, panel_ref, sums_ref, mass_ref, score_ref, held, more_vmem
+    steps, zn, few, slots, flag_ref, in_ref, more_ref, panel_ref, sums_ref, mass_ref, score_ref,
+    held, more_vmem,
 ):
     g = pl.program_id(0)
     pad = 2 * CAP
     tall = zn * pad
     width = in_ref.shape[1]
-    per, rest = in_ref.shape[0] // 2, more_vmem.shape[0] // 2
-    top = zn // 2
-
-    @pl.when(g < pairs)
+    deep, more_deep = in_ref.shape[0] // few, more_vmem.shape[0]
+    per, rest = deep // 2, more_deep // 2
+
+    def lay(block, dest, start, add):
+        pick = jnp.where(iota((tall, block.shape[0]), 0) == dest, 1.0, 0.0)
+        there = jnp.broadcast_to(jnp.sum(pick, axis=1, keepdims=True), (tall, 128))
+        laid = dot(pick.astype(BF), block)
+        for j in range(zn):
+            part = slice(j * pad, (j + 1) * pad)
+            for value, lanes in ((laid[part], slice(0, width)), (there[part], slice(width, width + 128))):
+                if add:
+                    value = value + held[j, pl.ds(start, pad), lanes].astype(F32)
+                held[j, pl.ds(start, pad), lanes] = value.astype(BF)
+
+    @pl.when(g < steps)
     def _():
-        notes = [in_ref[k * per - 1 : k * per, 0:128].astype(F32) for k in (1, 2)]
-        start = pl.multiple_of(g * pad, 16)
-
-        def lay(block, dest, add):
-            pick = jnp.where(iota((tall, block.shape[0]), 0) == dest, 1.0, 0.0)
-            there = jnp.broadcast_to(jnp.sum(pick, axis=1, keepdims=True), (tall, 128))
-            laid = dot(pick.astype(BF), block)
-            for j in range(zn):
-                part = slice(j * pad, (j + 1) * pad)
-                for value, lanes in ((laid[part], slice(0, width)), (there[part], slice(width, width + 128))):
-                    if add:
-                        value = value + held[j, pl.ds(start, pad), lanes].astype(F32)
-                    held[j, pl.ds(start, pad), lanes] = value.astype(BF)
-
-        lay(in_ref[...], places(zn, notes, per, 0, per - 1), False)
+        for k in range(few):
+            last = [k * deep + per - 1, (k + 1) * deep - 1]
+            notes = [in_ref[r : r + 1, 0:128].astype(F32) for r in last]
+            start = pl.multiple_of((g * few + k) * pad, 16)
+            block = in_ref[k * deep : (k + 1) * deep]
+            lay(block, places(zn, notes, per, 0, per - 1), start, False)
 
         @pl.when(flag_ref[0] != 0)
         def _():
-            deep = 2 * rest
-            pltpu.sync_copy(more_ref.at[pl.ds(pl.multiple_of(g * deep, 16), deep), :], more_vmem)
-            lay(more_vmem[...], places(zn, notes, rest, per - 1, rest), True)
-
-    @pl.when(g >= pairs)
+            @pl.loop(0, few)
+            def _(k):
+                pair = g * few + k
+                top = pl.multiple_of(k * deep, 16)
+                ends = [in_ref[pl.ds(pl.multiple_of(top + (h + 1) * per - 16, 16), 16), 0:128] for h in (0, 1)]
+                notes = [e.astype(F32)[15:16] for e in ends]
+                start = pl.multiple_of(pair * pad, 16)
+                from_row = pl.multiple_of(pair * more_deep, 16)
+                pltpu.sync_copy(more_ref.at[pl.ds(from_row, more_deep), :], more_vmem)
+                lay(more_vmem[...], places(zn, notes, rest, per - 1, rest), start, True)
+
+    @pl.when(g >= steps)
     def _():
-        j = g - pairs
-        x = held[j]
-        panel = panel_ref[0]
-        wide = panel.astype(F32)
-        sqnorm = jnp.sum(wide * wide, axis=1, keepdims=True)
-        logits = dot(panel, x[:, :width], ((1,), (1,))) - 0.5 * sqnorm
-        peak = jnp.max(logits, axis=0, keepdims=True)
-        shifted = jnp.exp(logits - peak)
-        total = jnp.sum(shifted, axis=0, keepdims=True)
-        score_ref[pl.ds(j, 1), :] = peak + jnp.log(total)
-        weights = (shifted * (1.0 / total)).astype(BF)
-        sums = dot(weights, x)
-        sums_ref[0] = sums[:, :width].astype(BF)
-        mass_ref[pl.ds(j, 1), :] = jnp.transpose(sums[:, width:])[0:1]
-
-
-def assign(flag, rows, more, panels, pairs):
+        first = (g - steps) * slots
+        logits = []
+        for k in range(slots):
+            panel = panel_ref[k]
+            wide = panel.astype(F32)
+            sqnorm = jnp.sum(wide * wide, axis=1, keepdims=True)
+            logits.append(dot(panel, held[first + k][:, :width], ((1,), (1,))) - 0.5 * sqnorm)
+        for k in range(slots):
+            peak = jnp.max(logits[k], axis=0, keepdims=True)
+            shifted = jnp.exp(logits[k] - peak)
+            total = jnp.sum(shifted, axis=0, keepdims=True)
+            score_ref[pl.ds(first + k, 1), :] = peak + jnp.log(total)
+            weights = (shifted * (1.0 / total)).astype(BF)
+            sums = dot(weights, held[first + k])
+            sums_ref[k] = sums[:, :width].astype(BF)
+            mass_ref[pl.ds(first + k, 1), :] = jnp.transpose(sums[:, width:])[0:1]
+
+
+def assign(flag, rows, more, panels, pairs, few=8, slots=2):
     zn, fine, width = panels.shape
     deep, more_deep = rows.shape[0] // pairs, more.shape[0] // pairs
     spread = pairs * 2 * CAP
-    last = pairs - 1
+    steps = pairs // few
     whole = lambda g, f: (0, 0)
+    by_slot = lambda g, f: (jnp.maximum(g - steps, 0), 0, 0)
     return pl.pallas_call(
-        functools.partial(assign_kernel, pairs, zn),
+        functools.partial(assign_kernel, steps, zn, few, slots),
         grid_spec=pltpu.PrefetchScalarGridSpec(
             num_scalar_prefetch=1,
-            grid=(pairs + zn,),
+            grid=(steps + zn // slots,),
             in_specs=[
-                pl.BlockSpec((deep, width), lambda g, f: (jnp.minimum(g, last), 0)),
+                pl.BlockSpec((few * deep, width), lambda g, f: (jnp.minimum(g, steps - 1), 0)),
                 pl.BlockSpec(memory_space=pl.ANY),
-                pl.BlockSpec((1, fine, width), lambda g, f: (jnp.maximum(g - pairs, 0), 0, 0)),
+                pl.BlockSpec((slots, fine, width), by_slot),
             ],
             out_specs=[
-                pl.BlockSpec((1, fine, width), lambda g, f: (jnp.maximum(g - pairs, 0), 0, 0)),
+                pl.BlockSpec((slots, fine, width), by_slot),
                 pl.BlockSpec((zn, fine), whole),
                 pl.BlockSpec((zn, spread), whole),
             ],
@@ -266,7 +279,7 @@
 
     panel = exchange(centroids, ("y", "x")).reshape(-1, width)
     place, note = index(
-        coarse_id.reshape(1, rows), owner_map.reshape(1, -1), zn, dpn, cores, bound, width
+        coarse_id.reshape(1, rows), owner_map.reshape(1, -1), zn, dpn, cores, bound
     )
     packed = pack(place, points, note, ROWS, 0, bound, 1024, True)
     arrived = exchange(packed.reshape(peers, ROWS, width), PLANE)

time: 219 us -> 240 us (1.096)
  starting transfers between devices: 37.5 us -> 70.5 us
  Pallas kernels: 45.1 us -> 34.8 us
    all_to_all x5, starting transfers between devices: 37.5 us -> 70.4 us  [exchange(): return lax.all_to_all(x, axes, split_axis=0, concat_axis=0, tiled=True)]
    pallas_call x1, Pallas kernels: 22.8 us -> 14.1 us  [assign(): pl.pallas_call(functools.partial(assign_kernel, steps, zn, few, slots), g...]
  transfers between devices with their start and end apart: 7 -> 7, of which waited for: 4 -> 4; matrix products, arithmetic and copies ran while one was open for 3% -> 3% of each run, Pallas kernels for 10% -> 9%
where the time goes in v3:
time: 240 us; the launch traced here: 241 us
  waiting for transfers between devices  111 us (46%)
  starting transfers between devices  70.5 us (29%)
  Pallas kernels  34.8 us (14%)
  between operations  15.4 us (6%)
  local copies, waits for them, and re-layouts  5.6 us (2%)
  other arithmetic  3.56 us (1%)
    all_to_all x5, waiting for transfers between devices, exchange(): return lax.all_to_all(x, axes, split_axis=0, concat_axis=0, tiled=True)  85.7 us
    all_to_all x5, starting transfers between devices, exchange(): return lax.all_to_all(x, axes, split_axis=0, concat_axis=0, tiled=True)  70.4 us
    reduce_scatter x1, waiting for transfers between devices, local(): sums = lax.psum_scatter(sums, 'z', scatter_dimension=0, tiled=True)[0]  24.5 us
    pallas_call x1, Pallas kernels, pack(): pl.pallas_call(functools.partial(pack_kernel, per, first, bound, noted),...  15.7 us
    pallas_call x1, Pallas kernels, assign(): pl.pallas_call(functools.partial(assign_kernel, steps, zn, few, slots), g...  14.1 us
  transfers between devices with their start and end apart: 7, of which 4 were waited for; matrix products, arithmetic and copies ran while one was open for 3% of the time, Pallas kernels for 9%

profile of v3, /device:TPU:2, one launch (start us, length us, event | category | flops | bytes accessed | tf_op | source)
XLA Modules:
  0.0 240.9 jit_solution(10250944145223226584)
XLA Ops:
  7.2 0.0 copy-start.2
  7.2 7.8 %all-to-all-start.3 = ((bf16[16,16,768]{2,1,0:T(8,128)(2,1)}), bf16[16,16,768]{2,1,0:T(8,128)(2,1)S(1)}, u32[]{:S(2)}, u32[]{:S(2)}) async-start(bf16[16,16,768]{2,1,0:T(8,128)(2,1)} %param.10), calls=%async_computation.3 | async-start | bytes 786432 | tf_op jit(solution)/shard_map/all_to_all | solution.py:270
  14.9 2.9 %place.1 = (s32[8,2048]{1,0:T(8,128)}, f32[32,128]{1,0:T(8,128)S(1)}) custom-call(s32[1,2048]{1,0:T(1,128)} %bitcast.26, s32[1,256]{1,0:T(1,128)} %bitcast.27), custom_call_target="tpu_custom_call" | custom-call | flops 1000000000 | bytes 100000 | tf_op jit(solution)/shard_map/place/pallas_call | solution.py:74
  17.9 0.0 copy-done.2
  17.9 15.7 %pack.5 = bf16[4096,768]{1,0:T(8,128)(2,1)} custom-call(s32[8,2048]{1,0:T(8,128)} %get-tuple-element.29.place_ref, bf16[2048,768]{1,0:T(8,128)(2,1)S(1)} %copy-done.2, f32[32,128]{1,0:T(8,128)S(1)} %get-tuple-element.30.note_ref), custom_call_target="tpu_custom_call" | custom-call | flops 12884901888 | bytes 10000000 | tf_op jit(solution)/shard_map/pack/pallas_call | solution.py:106
  33.6 0.0 all-to-all-done.3
  33.6 0.0 copy-start
  33.6 0.7 copy-done
  34.3 7.4 %all-to-all-start.2 = ((bf16[32,128,768]{2,1,0:T(8,128)(2,1)}), bf16[32,128,768]{2,1,0:T(8,128)(2,1)}, u32[]{:S(2)}, u32[]{:S(2)}) async-start(bf16[32,128,768]{2,1,0:T(8,128)(2,1)} %bitcast.16), calls=%async_computation.2 | async-start | bytes 12582912 | tf_op jit(solution)/shard_map/all_to_all | solution.py:270
  41.8 0.0 all-gather.2.cloned.1.call-start
  41.8 0.7 all-gather.2.cloned.1.call-update
  42.5 0.0 reduce-scatter.2.cloned.1.call-start
  42.5 74.4 %all-to-all-done.2 = bf16[32,128,768]{2,1,0:T(8,128)(2,1)} async-done(((bf16[32,128,768]{2,1,0:T(8,128)(2,1)}), bf16[32,128,768]{2,1,0:T(8,128)(2,1)}, u32[]{:S(2)}, u32[]{:S(2)}) %all-to-all-start.2) | async-done | bytes 6291488 | tf_op jit(solution)/shard_map/all_to_all | solution.py:270
  117.0 1.6 slice_reduce_fusion
  119.8 0.4 conditional.1
  119.8 0.2 broadcast.12
  120.3 0.0 all-gather.2.cloned.1.call-done.panel_ref
  120.3 14.1 %assign.1 = (bf16[8,256,768]{2,1,0:T(8,128)(2,1)}, f32[8,256]{1,0:T(8,128)}, f32[8,768]{1,0:T(8,128)}) custom-call(s32[1]{0:T(128)} %bitcast.7.flag_ref, bf16[4096,768]{1,0:T(8,128)(2,1)} %bitcast.8.in_ref, bf16[2304,768]{1,0:T(8,128)(2,1)S(1)} %get-tuple-element.38.more_ref, bf16[8,256,768]{2,1,0:T(8,128)(2,1)} %all-gather.2.cloned.1.call-done.panel_ref), custom_call_target="tpu_custom_call" | custom-call | flops 8000000000 | bytes 20000000 | tf_op jit(solution)/shard_map/assign/pallas_call | solution.py:215
  134.4 0.0 copy-start.1
  134.4 0.0 copy-start.3
  134.4 0.0 reduce-scatter.2.cloned.1.call-update
  134.4 1.3 copy.8
  135.7 42.8 %all-to-all-start.4 = ((f32[8,1,256]{2,1,0:T(1,128)}), f32[8,1,256]{2,1,0:T(1,128)S(1)}, u32[]{:S(2)}, u32[]{:S(2)}) async-start(f32[8,1,256]{2,1,0:T(1,128)} %copy.8), calls=%async_computation.5 | async-start | bytes 16384 | tf_op jit(solution)/shard_map/all_to_all | solution.py:270
  178.5 0.8 reshape.69
  179.3 0.1 copy.9
  179.4 0.8 all_to_all.34
  180.2 6.2 %all-to-all-done.4 = f32[8,1,256]{2,1,0:T(1,128)S(1)} async-done(((f32[8,1,256]{2,1,0:T(1,128)}), f32[8,1,256]{2,1,0:T(1,128)S(1)}, u32[]{:S(2)}, u32[]{:S(2)}) %all-to-all-start.4) | async-done | bytes 8224 | tf_op jit(solution)/shard_map/all_to_all | solution.py:270
  186.3 5.0 %all-to-all-start.6 = ((f32[32,1,192]{2,1,0:T(1,128)}), f32[32,1,192]{2,1,0:T(1,128)S(1)}, u32[]{:S(2)}, u32[]{:S(2)}) async-start(f32[32,1,192]{2,1,0:T(1,128)} %all_to_all.34), calls=%async_computation.7 | async-start | bytes 65536 | tf_op jit(solution)/shard_map/all_to_all | solution.py:270
  191.4 0.1 add.29
  191.5 24.5 %reduce-scatter.2.cloned.1.call-done = bf16[1,256,768]{2,1,0:T(8,128)(2,1)} async-done(((bf16[8,256,768]{2,1,0:T(8,128)(2,1)}), bf16[1,256,768]{2,1,0:T(8,128)(2,1)}) %reduce-scatter.2.cloned.1.call-update) | async-done | bytes 393232 | tf_op jit(solution)/shard_map/reduce_scatter | solution.py:303
  216.0 0.0 copy-done.1
  216.0 1.9 fusion.1
  217.9 0.0 all-to-all-done.6
  217.9 7.4 %all-to-all-start.5 = ((bf16[16,16,768]{2,1,0:T(8,128)(2,1)}), bf16[16,16,768]{2,1,0:T(8,128)(2,1)S(1)}, u32[]{:S(2)}, u32[]{:S(2)}) async-start(bf16[16,16,768]{2,1,0:T(8,128)(2,1)} %fusion.1), calls=%async_computation.6 | async-start | bytes 786432 | tf_op jit(solution)/shard_map/all_to_all | solution.py:270
  225.3 0.1 reduce.3
  225.4 0.1 reshape.70
  225.5 0.7 copy.11
  226.1 0.0 copy-done.3
  226.2 2.1 lookup.1
  228.2 5.1 %all-to-all-done.5 = bf16[16,16,768]{2,1,0:T(8,128)(2,1)S(1)} async-done(((bf16[16,16,768]{2,1,0:T(8,128)(2,1)}), bf16[16,16,768]{2,1,0:T(8,128)(2,1)S(1)}, u32[]{:S(2)}, u32[]{:S(2)}) %all-to-all-start.5) | async-done | bytes 393248 | tf_op jit(solution)/shard_map/all_to_all | solution.py:270
  233.3 0.7 copy.16
  (2 shorter events, 0.0 us)
Async XLA Ops:
  7.2 10.7 %copy-start.2 = (bf16[2048,768]{1,0:T(8,128)(2,1)S(1)}, bf16[2048,768]{1,0:T(8,128)(2,1)}, u32[]{:S(2)}) copy-start(bf16[2048,768]{1,0:T(8,128)(2,1)} %points_ref.1) | copy-start | bytes 9437188
  7.2 26.4 %all-to-all-start.3 = ((bf16[16,16,768]{2,1,0:T(8,128)(2,1)}), bf16[16,16,768]{2,1,0:T(8,128)(2,1)S(1)}, u32[]{:S(2)}, u32[]{:S(2)}) async-start(bf16[16,16,768]{2,1,0:T(8,128)(2,1)} %param.10), calls=%async_computation.3 | async-start | bytes 786432 | tf_op jit(solution)/shard_map/all_to_all | solution.py:270
  33.6 0.7 copy-start
  34.3 82.6 %all-to-all-start.2 = ((bf16[32,128,768]{2,1,0:T(8,128)(2,1)}), bf16[32,128,768]{2,1,0:T(8,128)(2,1)}, u32[]{:S(2)}, u32[]{:S(2)}) async-start(bf16[32,128,768]{2,1,0:T(8,128)(2,1)} %bitcast.16), calls=%async_computation.2 | async-start | bytes 12582912 | tf_op jit(solution)/shard_map/all_to_all | solution.py:270
  41.8 78.5 %all-gather.2.cloned.1.call-start = ((), (), s32[]{:S(2)}) async-start(), calls=%async_computation.8 | async-start | bytes 3538944 | tf_op jit(solution)/shard_map/all_gather | solution.py:286
  42.5 173.5 %reduce-scatter.2.cloned.1.call-start = ((), (), s32[]{:S(2)}) async-start(), calls=%async_computation.9 | async-start | bytes 3538944 | tf_op jit(solution)/shard_map/reduce_scatter | solution.py:303
  134.4 81.6 %copy-start.1 = (bf16[16,16,768]{2,1,0:T(8,128)(2,1)S(1)}, bf16[16,16,768]{2,1,0:T(8,128)(2,1)}, u32[]{:S(2)}) copy-start(bf16[16,16,768]{2,1,0:T(8,128)(2,1)} %copy-done) | copy-start | bytes 1179652
  134.4 91.8 %copy-start.3 = (s32[8,2048]{1,0:T(8,128)S(1)}, s32[8,2048]{1,0:T(8,128)}, u32[]{:S(2)}) copy-start(s32[8,2048]{1,0:T(8,128)} %get-tuple-element.29.place_ref) | copy-start | bytes 196612
  135.7 50.6 %all-to-all-start.4 = ((f32[8,1,256]{2,1,0:T(1,128)}), f32[8,1,256]{2,1,0:T(1,128)S(1)}, u32[]{:S(2)}, u32[]{:S(2)}) async-start(f32[8,1,256]{2,1,0:T(1,128)} %copy.8), calls=%async_computation.5 | async-start | bytes 16384 | tf_op jit(solution)/shard_map/all_to_all | solution.py:270
  186.3 31.5 %all-to-all-start.6 = ((f32[32,1,192]{2,1,0:T(1,128)}), f32[32,1,192]{2,1,0:T(1,128)S(1)}, u32[]{:S(2)}, u32[]{:S(2)}) async-start(f32[32,1,192]{2,1,0:T(1,128)} %all_to_all.34), calls=%async_computation.7 | async-start | bytes 65536 | tf_op jit(solution)/shard_map/all_to_all | solution.py:270
  217.9 15.5 %all-to-all-start.5 = ((bf16[16,16,768]{2,1,0:T(8,128)(2,1)}), bf16[16,16,768]{2,1,0:T(8,128)(2,1)S(1)}, u32[]{:S(2)}, u32[]{:S(2)}) async-start(bf16[16,16,768]{2,1,0:T(8,128)(2,1)} %fusion.1), calls=%async_computation.6 | async-start | bytes 786432 | tf_op jit(solution)/shard_map/all_to_all | solution.py:270
Sparse Core Ops, SparseCore 0:
  44.9 47.6 all-gather.1
  134.5 81.4 reduce-scatter.1

commit v4 on v3

--- a/solution.py
+++ b/solution.py
@@ -9,6 +9,8 @@
 PRIOR = 4.0
 CAP = 24
 ROWS = 128
+BLOCK = 256
+WINDOW = 64
 SOME, REST = 16, 72
 PLANE = ("y", "x", "core")
 BF = jnp.bfloat16
@@ -27,42 +29,58 @@
     return jnp.where(mask, 1.0, 0.0).astype(BF)
 
 
-def index_kernel(zn, dpn, cores, bound, coarse_ref, owner_ref, place_ref, note_ref, hot_ref):
+def index_kernel(
+    zn, dpn, cores, bound, coarse_ref, owner_ref, place_ref, note_ref, segment_ref, hot_ref
+):
     slots = owner_ref.shape[1]
     rows = coarse_ref.shape[1]
+    blocks = rows // BLOCK
     peers, width = note_ref.shape
     owner = owner_ref[...]
     column, cluster = owner % dpn, owner // dpn
     lane_of = (column * cores + cluster % cores) * zn + cluster // cores
     move = onehot(iota((slots, slots), 0) == lane_of)
-    blk = 256
-    earlier = onehot(iota((blk, blk), 0) < iota((blk, blk), 1))
-    carry = jnp.zeros((slots, 1), F32)
-    ranks = []
-    for b in range(rows // blk):
-        named = onehot(iota((slots, blk), 0) == coarse_ref[:, b * blk : (b + 1) * blk])
+    earlier = onehot(iota((BLOCK, BLOCK), 0) < iota((BLOCK, BLOCK), 1))
+    ranks, sizes = [], []
+    for b in range(blocks):
+        part = slice(b * BLOCK, (b + 1) * BLOCK)
+        named = onehot(iota((slots, BLOCK), 0) == coarse_ref[:, part])
         hot = dot(move, named)
         hot_bf = hot.astype(BF)
-        hot_ref[:, b * blk : (b + 1) * blk] = hot_bf
-        before = dot(hot_bf, earlier) + carry
-        ranks.append(jnp.sum(hot * before, axis=0, keepdims=True))
-        carry = carry + jnp.sum(hot, axis=1, keepdims=True)
+        hot_ref[:, part] = hot_bf
+        ranks.append(jnp.sum(hot * dot(hot_bf, earlier), axis=0, keepdims=True))
+        sizes.append(dot(jnp.ones((8, BLOCK), BF), hot_bf, ((1,), (1,)))[0:1])
     rank = jnp.concatenate(ranks, axis=1)
-    hot_all = hot_ref[...]
-    counts = dot(jnp.ones((8, rows), BF), hot_all, ((1,), (1,)))
+    size = jnp.concatenate(sizes, axis=0)
+    done, carry = jnp.zeros((1, slots), F32), []
+    for b in range(blocks):
+        carry.append(done)
+        done = done + sizes[b]
+    carry = jnp.concatenate(carry, axis=0)
     la, lb = iota((slots, slots), 0), iota((slots, slots), 1)
+    lower = dot(size.astype(BF), onehot(la < lb))
     group = onehot((la // zn == lb // zn) & (la < lb))
-    offset = dot(counts.astype(BF), group)
+    offset = dot(jnp.broadcast_to(done, (8, slots)).astype(BF), group)
     which = iota((8, slots), 0)
-    query = jnp.where(which == 0, offset, iota((8, slots), 1).astype(F32)).astype(BF)
-    found = dot(query, hot_all)
+    query = jnp.where(which == 0, offset, iota((8, slots), 1).astype(F32))
+    query = jnp.concatenate([query, lower, carry], axis=0).astype(BF)
+    found = dot(query, hot_ref[...])
+    own = iota((blocks, rows), 1) // BLOCK == iota((blocks, rows), 0)
+    mine = lambda k: jnp.sum(
+        jnp.where(own, found[8 + k * blocks : 8 + (k + 1) * blocks], 0.0), axis=0, keepdims=True
+    )
+    sort = (rank + mine(0)).astype(jnp.int32)
+    rank = (rank + mine(1)).astype(jnp.int32)
     lane = found[1:2].astype(jnp.int32)
-    rank = rank.astype(jnp.int32)
     pos = (lane // zn) * bound + found[0:1].astype(jnp.int32) + rank
     row = iota((8, rows), 0)
-    place_ref[...] = jnp.where(row == 0, pos, jnp.where(row == 1, lane, rank))
+    place_ref[...] = jnp.where(
+        row == 0, pos, jnp.where(row == 1, lane, jnp.where(row == 2, rank, sort))
+    )
+    segment_ref[:, :slots] = lower.astype(jnp.int32)
+    segment_ref[:, slots:] = jnp.full((blocks, 128), BLOCK, jnp.int32)
     mine = iota((peers, slots), 1) // zn == iota((peers, slots), 0)
-    spread = jnp.where(mine, counts[0:1], 0.0)
+    spread = jnp.where(mine, done, 0.0)
     most = jnp.max(jnp.sum(spread, axis=1, keepdims=True), axis=0, keepdims=True)
     spot = onehot(iota((slots, width), 0) % zn == iota((slots, width), 1))
     note = dot(spread.astype(BF), spot)
@@ -76,6 +94,7 @@
         out_shape=(
             jax.ShapeDtypeStruct((8, rows), jnp.int32),
             jax.ShapeDtypeStruct((dpn * cores, 128), F32),
+            jax.ShapeDtypeStruct((rows // BLOCK, slots + 128), jnp.int32),
         ),
         scratch_shapes=[pltpu.VMEM((slots, rows), BF)],
         cost_estimate=pl.CostEstimate(flops=10**9, bytes_accessed=10**5, transcendentals=0),
@@ -83,33 +102,23 @@
     )(coarse, owner)
 
 
-def pack_kernel(per, first, bound, noted, place_ref, points_ref, note_ref, out_ref):
+def pack_kernel(per, first, bound, place_ref, points_ref, out_ref):
     g = pl.program_id(0)
-    tall, width = out_ref.shape
+    tall = out_ref.shape[0]
     i = iota((tall, 1), 0)
-    peer, at = g * (tall // per) + i // per, i % per
-    want = peer * bound + first + at
+    want = (g * (tall // per) + i // per) * bound + first + i % per
     pick = onehot(place_ref[0:1, :] == want)
-    packed = dot(pick, points_ref[...])
-    out_ref[...] = packed.astype(BF)
-    if noted:
-        for k in range(tall // per):
-            tile = slice((k + 1) * per - 16, (k + 1) * per)
-            note = jnp.broadcast_to(note_ref[k : k + 1], (16, 128))
-            end = iota((16, 128), 0) == 15
-            out_ref[tile, :128] = jnp.where(end, note, packed[tile, :128]).astype(BF)
-
-
-def pack(place, points, note, per, first, bound, tall, noted):
+    out_ref[...] = dot(pick, points_ref[...]).astype(BF)
+
+
+def pack(place, points, peers, per, first, bound, tall):
     rows, width = points.shape
-    peers = note.shape[0]
     return pl.pallas_call(
-        functools.partial(pack_kernel, per, first, bound, noted),
+        functools.partial(pack_kernel, per, first, bound),
         grid=(peers * per // tall,),
         in_specs=[
             pl.BlockSpec((8, rows), lambda g: (0, 0)),
             pl.BlockSpec((rows, width), lambda g: (0, 0)),
-            pl.BlockSpec((tall // per, 128), lambda g: (g, 0)),
         ],
         out_specs=pl.BlockSpec((tall, width), lambda g: (g, 0)),
         out_shape=jax.ShapeDtypeStruct((peers * per, width), BF),
@@ -117,7 +126,109 @@
             flops=2 * peers * per * rows * width, bytes_accessed=10**7, transcendentals=0
         ),
         name="pack",
-    )(place, points, note)
+    )(place, points)
+
+
+def sort_pack_kernel(
+    per, bound, zn, segment_ref, place_ref, points_ref, note_ref, out_ref, sorted_ref, key_ref,
+    near_ref,
+):
+    g = pl.program_id(0)
+    tall = out_ref.shape[0]
+    blocks = points_ref.shape[0] // BLOCK
+    wide = BLOCK // WINDOW
+
+    @pl.when(g == 0)
+    def _():
+        for b in range(blocks):
+            part = slice(b * BLOCK, (b + 1) * BLOCK)
+            move = onehot(iota((BLOCK, BLOCK), 0) == place_ref[3:4, part])
+            sorted_ref[part] = dot(move, points_ref[part]).astype(BF)
+            key = place_ref[0:1, part]
+            which = iota((8, BLOCK), 0)
+            halves = jnp.where(which == 0, key // 128, jnp.where(which == 1, key % 128, 0))
+            keys = dot(halves.astype(F32).astype(BF), move, ((1,), (1,)))
+            key_ref[b : b + 1, :] = (keys[0:1] * 128.0 + keys[1:2]).astype(jnp.int32)
+
+    both = 2 * per
+    i = iota((both, 1), 0)
+    lane = iota((1, BLOCK), 1)
+
+    def picked(q, group, starts, news):
+        want = (group * 2 + i // per) * bound + i % per
+        keys = []
+        for b in range(blocks):
+            rows = pl.multiple_of(b * BLOCK + starts[b], 16)
+            near_ref[q, b * WINDOW : (b + 1) * WINDOW, :] = sorted_ref[pl.ds(rows, WINDOW), :]
+            key = key_ref[b : b + 1, :]
+            if news is not None:
+                key = jnp.where(lane >= news[b], key, -1)
+            shift = (b % wide) * WINDOW + BLOCK - starts[b]
+            key = pltpu.roll(key, shift % BLOCK, 1)
+            if b % wide == 0:
+                keys.append(key)
+            else:
+                keys[-1] = jnp.where(lane >= (b % wide) * WINDOW, key, keys[-1])
+        pick = onehot(jnp.concatenate(keys, axis=1) == want)
+        return dot(pick, near_ref[q])
+
+    groups = tall // both
+    longest, lows_of = jnp.int32(0), []
+    for q in range(groups):
+        first = (g * groups + q) * 2 * zn
+        lows = [segment_ref[b, first] // 16 * 16 for b in range(blocks)]
+        highs = [segment_ref[b, first + 2 * zn] for b in range(blocks)]
+        for low, high in zip(lows, highs):
+            longest = jnp.maximum(longest, high - low)
+        lows_of.append(lows)
+        starts = [jnp.minimum(low, BLOCK - WINDOW) for low in lows]
+        out_ref[q * both : (q + 1) * both] = picked(q, g * groups + q, starts, None).astype(BF)
+
+    @pl.when(longest > WINDOW)
+    def _():
+        @pl.loop(1, (longest + WINDOW - 1) // WINDOW)
+        def _(w):
+            for q in range(groups):
+                here = slice(q * both, (q + 1) * both)
+                news = [low + w * WINDOW for low in lows_of[q]]
+                starts = [jnp.minimum(new, BLOCK - WINDOW) for new in news]
+                more = picked(q, g * groups + q, starts, news)
+                out_ref[here] = (out_ref[here].astype(F32) + more).astype(BF)
+
+    for k in range(tall // per):
+        tile = slice((k + 1) * per - 16, (k + 1) * per)
+        note = jnp.broadcast_to(note_ref[k : k + 1], (16, 128))
+        end = iota((16, 128), 0) == 15
+        out_ref[tile, :128] = jnp.where(end, note, out_ref[tile, :128].astype(F32)).astype(BF)
+
+
+def sort_pack(segment, place, points, note, per, bound, zn, tall):
+    rows, width = points.shape
+    peers = note.shape[0]
+    blocks = rows // BLOCK
+    return pl.pallas_call(
+        functools.partial(sort_pack_kernel, per, bound, zn),
+        grid_spec=pltpu.PrefetchScalarGridSpec(
+            num_scalar_prefetch=1,
+            grid=(peers * per // tall,),
+            in_specs=[
+                pl.BlockSpec((8, rows), lambda g, s: (0, 0)),
+                pl.BlockSpec((rows, width), lambda g, s: (0, 0)),
+                pl.BlockSpec((tall // per, 128), lambda g, s: (g, 0)),
+            ],
+            out_specs=pl.BlockSpec((tall, width), lambda g, s: (g, 0)),
+            scratch_shapes=[
+                pltpu.VMEM((rows, width), BF),
+                pltpu.VMEM((blocks, BLOCK), jnp.int32),
+                pltpu.VMEM((tall // (2 * per), blocks * WINDOW, width), BF),
+            ],
+        ),
+        out_shape=jax.ShapeDtypeStruct((peers * per, width), BF),
+        cost_estimate=pl.CostEstimate(
+            flops=5 * 10**9, bytes_accessed=10**7, transcendentals=0
+        ),
+        name="sort_pack",
+    )(segment, place, points, note)
 
 
 def places(zn, notes, per, first, count):
@@ -149,7 +260,7 @@
     pad = 2 * CAP
     tall = zn * pad
     width = in_ref.shape[1]
-    deep, more_deep = in_ref.shape[0] // few, more_vmem.shape[0]
+    deep, more_deep = in_ref.shape[0] // few, more_vmem.shape[0] // (steps * few)
     per, rest = deep // 2, more_deep // 2
 
     def lay(block, dest, start, add):
@@ -174,6 +285,10 @@
 
         @pl.when(flag_ref[0] != 0)
         def _():
+            @pl.when(g == 0)
+            def _():
+                pltpu.sync_copy(more_ref, more_vmem)
+
             @pl.loop(0, few)
             def _(k):
                 pair = g * few + k
@@ -182,8 +297,7 @@
                 notes = [e.astype(F32)[15:16] for e in ends]
                 start = pl.multiple_of(pair * pad, 16)
                 from_row = pl.multiple_of(pair * more_deep, 16)
-                pltpu.sync_copy(more_ref.at[pl.ds(from_row, more_deep), :], more_vmem)
-                lay(more_vmem[...], places(zn, notes, rest, per - 1, rest), start, True)
+                lay(more_vmem[pl.ds(from_row, more_deep), :], places(zn, notes, rest, per - 1, rest), start, True)
 
     @pl.when(g >= steps)
     def _():
@@ -207,7 +321,7 @@
 
 def assign(flag, rows, more, panels, pairs, few=8, slots=2):
     zn, fine, width = panels.shape
-    deep, more_deep = rows.shape[0] // pairs, more.shape[0] // pairs
+    deep = rows.shape[0] // pairs
     spread = pairs * 2 * CAP
     steps = pairs // few
     whole = lambda g, f: (0, 0)
@@ -229,7 +343,7 @@
             ],
             scratch_shapes=[
                 pltpu.VMEM((zn, spread, width + 128), BF),
-                pltpu.VMEM((more_deep, width), BF),
+                pltpu.VMEM(more.shape, BF),
             ],
         ),
         out_shape=(
@@ -278,17 +392,17 @@
     rows, width = points.shape
 
     panel = exchange(centroids, ("y", "x")).reshape(-1, width)
-    place, note = index(
+    place, note, segment = index(
         coarse_id.reshape(1, rows), owner_map.reshape(1, -1), zn, dpn, cores, bound
     )
-    packed = pack(place, points, note, ROWS, 0, bound, 1024, True)
+    packed = sort_pack(segment, place, points, note, ROWS, bound, zn, 1024)
     arrived = exchange(packed.reshape(peers, ROWS, width), PLANE)
     panels = lax.all_gather(panel, "z", axis=0)
 
     most = jnp.max(arrived[:, ROWS - 1, zn].astype(F32))
 
     def second(per):
-        block = pack(place, points, note, per, ROWS - 1, bound, 16 * per, False)
+        block = pack(place, points, peers, per, ROWS - 1, bound, 16 * per)
         block = exchange(block.reshape(peers, per, width), PLANE)
         return jnp.pad(block, ((0, 0), (0, REST - per), (0, 0))).reshape(peers * REST, width)
 

time: 240 us -> 202 us (0.84)
  starting transfers between devices: 70.5 us -> 37.7 us
  Pallas kernels: 34.8 us -> 28.1 us
    all_to_all x5, starting transfers between devices: 70.4 us -> 37.6 us  [exchange(): return lax.all_to_all(x, axes, split_axis=0, concat_axis=0, tiled=True)]
    pallas_call x1, Pallas kernels: 15.7 us -> 8.67 us  [sort_pack(): pl.pallas_call(functools.partial(sort_pack_kernel, per, bound, zn), grid_...]
  transfers between devices with their start and end apart: 7 -> 7, of which waited for: 4 -> 4; matrix products, arithmetic and copies ran while one was open for 3% -> 3% of each run, Pallas kernels for 9% -> 7%
where the time goes in v4:
time: 202 us; the launch traced here: 201 us
  waiting for transfers between devices  110 us (54%)
  starting transfers between devices  37.7 us (19%)
  Pallas kernels  28.1 us (14%)
  between operations  15.4 us (8%)
  local copies, waits for them, and re-layouts  5.6 us (3%)
  other arithmetic  3.56 us (2%)
    all_to_all x5, waiting for transfers between devices, exchange(): return lax.all_to_all(x, axes, split_axis=0, concat_axis=0, tiled=True)  85.7 us
    all_to_all x5, starting transfers between devices, exchange(): return lax.all_to_all(x, axes, split_axis=0, concat_axis=0, tiled=True)  37.6 us
    reduce_scatter x1, waiting for transfers between devices, local(): sums = lax.psum_scatter(sums, 'z', scatter_dimension=0, tiled=True)[0]  23.9 us
    pallas_call x1, Pallas kernels, assign(): pl.pallas_call(functools.partial(assign_kernel, steps, zn, few, slots), g...  14 us
    pallas_call x1, Pallas kernels, sort_pack(): pl.pallas_call(functools.partial(sort_pack_kernel, per, bound, zn), grid_...  8.67 us
  transfers between devices with their start and end apart: 7, of which 4 were waited for; matrix products, arithmetic and copies ran while one was open for 3% of the time, Pallas kernels for 7%

profile of v4, /device:TPU:2, one launch (start us, length us, event | category | flops | bytes accessed | tf_op | source)
XLA Modules:
  0.0 200.9 jit_solution(9576788805119724149)
XLA Ops:
  7.2 0.0 copy-start.2
  7.2 7.8 %all-to-all-start.3 = ((bf16[16,16,768]{2,1,0:T(8,128)(2,1)}), bf16[16,16,768]{2,1,0:T(8,128)(2,1)S(1)}, u32[]{:S(2)}, u32[]{:S(2)}) async-start(bf16[16,16,768]{2,1,0:T(8,128)(2,1)} %param.10), calls=%async_computation.3 | async-start | bytes 786432 | tf_op jit(solution)/shard_map/all_to_all | solution.py:384
  14.9 3.4 %place.1 = (s32[8,2048]{1,0:T(8,128)}, f32[32,128]{1,0:T(8,128)}, s32[8,384]{1,0:T(8,128)}) custom-call(s32[1,2048]{1,0:T(1,128)} %bitcast.26, s32[1,256]{1,0:T(1,128)} %bitcast.27), custom_call_target="tpu_custom_call" | custom-call | flops 1000000000 | bytes 100000 | tf_op jit(solution)/shard_map/place/pallas_call | solution.py:92
  18.3 0.0 copy-done.2
  18.3 8.7 %sort_pack.1 = bf16[4096,768]{1,0:T(8,128)(2,1)} custom-call(s32[8,384]{1,0:T(8,128)} %get-tuple-element.24.segment_ref, s32[8,2048]{1,0:T(8,128)} %get-tuple-element.25.place_ref, bf16[2048,768]{1,0:T(8,128)(2,1)S(1)} %copy-done.2, f32[32,128]{1,0:T(8,128)} %get-tuple-element.26.note_ref), custom_call_target="tpu_custom_call" | custom-call | flops 5000000000 | bytes 10000000 | tf_op jit(solution)/shard_map/sort_pack/pallas_call | solution.py:209
  27.0 0.0 all-to-all-done.3
  27.0 0.0 copy-start
  27.0 0.7 copy-done
  27.7 7.4 %all-to-all-start.2 = ((bf16[32,128,768]{2,1,0:T(8,128)(2,1)}), bf16[32,128,768]{2,1,0:T(8,128)(2,1)}, u32[]{:S(2)}, u32[]{:S(2)}) async-start(bf16[32,128,768]{2,1,0:T(8,128)(2,1)} %bitcast.16), calls=%async_computation.2 | async-start | bytes 12582912 | tf_op jit(solution)/shard_map/all_to_all | solution.py:384
  35.1 0.0 all-gather.2.cloned.1.call-start
  35.2 0.7 all-gather.2.cloned.1.call-update
  35.9 0.0 reduce-scatter.2.cloned.1.call-start
  35.9 74.4 %all-to-all-done.2 = bf16[32,128,768]{2,1,0:T(8,128)(2,1)} async-done(((bf16[32,128,768]{2,1,0:T(8,128)(2,1)}), bf16[32,128,768]{2,1,0:T(8,128)(2,1)}, u32[]{:S(2)}, u32[]{:S(2)}) %all-to-all-start.2) | async-done | bytes 6291488 | tf_op jit(solution)/shard_map/all_to_all | solution.py:384
  110.3 1.6 slice_reduce_fusion
  113.2 0.4 conditional.1
  113.2 0.2 broadcast.12
  113.7 0.0 all-gather.2.cloned.1.call-done.panel_ref
  113.7 14.0 %assign.1 = (bf16[8,256,768]{2,1,0:T(8,128)(2,1)}, f32[8,256]{1,0:T(8,128)}, f32[8,768]{1,0:T(8,128)}) custom-call(s32[1]{0:T(128)} %bitcast.7.flag_ref, bf16[4096,768]{1,0:T(8,128)(2,1)} %bitcast.8.in_ref, bf16[2304,768]{1,0:T(8,128)(2,1)S(1)} %get-tuple-element.34.more_ref, bf16[8,256,768]{2,1,0:T(8,128)(2,1)} %all-gather.2.cloned.1.call-done.panel_ref), custom_call_target="tpu_custom_call" | custom-call | flops 8000000000 | bytes 20000000 | tf_op jit(solution)/shard_map/assign/pallas_call | solution.py:329
  127.7 0.0 copy-start.1
  127.7 0.0 copy-start.3
  127.7 0.0 reduce-scatter.2.cloned.1.call-update
  127.7 1.3 copy.8
  129.0 8.5 %all-to-all-start.4 = ((f32[8,1,256]{2,1,0:T(1,128)}), f32[8,1,256]{2,1,0:T(1,128)S(1)}, u32[]{:S(2)}, u32[]{:S(2)}) async-start(f32[8,1,256]{2,1,0:T(1,128)} %copy.8), calls=%async_computation.5 | async-start | bytes 16384 | tf_op jit(solution)/shard_map/all_to_all | solution.py:384
  137.5 0.8 reshape.69
  138.4 0.1 copy.9
  138.5 0.8 all_to_all.34
  139.2 6.1 %all-to-all-done.4 = f32[8,1,256]{2,1,0:T(1,128)S(1)} async-done(((f32[8,1,256]{2,1,0:T(1,128)}), f32[8,1,256]{2,1,0:T(1,128)S(1)}, u32[]{:S(2)}, u32[]{:S(2)}) %all-to-all-start.4) | async-done | bytes 8224 | tf_op jit(solution)/shard_map/all_to_all | solution.py:384
  145.3 6.6 %all-to-all-start.6 = ((f32[32,1,192]{2,1,0:T(1,128)}), f32[32,1,192]{2,1,0:T(1,128)S(1)}, u32[]{:S(2)}, u32[]{:S(2)}) async-start(f32[32,1,192]{2,1,0:T(1,128)} %all_to_all.34), calls=%async_computation.7 | async-start | bytes 65536 | tf_op jit(solution)/shard_map/all_to_all | solution.py:384
  151.9 0.1 add.29
  152.0 23.9 %reduce-scatter.2.cloned.1.call-done = bf16[1,256,768]{2,1,0:T(8,128)(2,1)} async-done(((bf16[8,256,768]{2,1,0:T(8,128)(2,1)}), bf16[1,256,768]{2,1,0:T(8,128)(2,1)}) %reduce-scatter.2.cloned.1.call-update) | async-done | bytes 393232 | tf_op jit(solution)/shard_map/reduce_scatter | solution.py:417
  175.9 0.0 copy-done.1
  175.9 1.9 fusion.1
  177.8 0.0 all-to-all-done.6
  177.8 7.5 %all-to-all-start.5 = ((bf16[16,16,768]{2,1,0:T(8,128)(2,1)}), bf16[16,16,768]{2,1,0:T(8,128)(2,1)S(1)}, u32[]{:S(2)}, u32[]{:S(2)}) async-start(bf16[16,16,768]{2,1,0:T(8,128)(2,1)} %fusion.1), calls=%async_computation.6 | async-start | bytes 786432 | tf_op jit(solution)/shard_map/all_to_all | solution.py:384
  185.3 0.1 reduce.3
  185.3 0.1 reshape.70
  185.5 0.7 copy.11
  186.1 0.0 copy-done.3
  186.1 2.1 %lookup.1 = f32[1,2048]{1,0:T(1,128)} custom-call(s32[8,2048]{1,0:T(8,128)S(1)} %copy-done.3, f32[24,256]{1,0:T(8,128)} %bitcast.24), custom_call_target="tpu_custom_call" | custom-call | flops 100000000 | bytes 100000 | tf_op jit(solution)/shard_map/lookup/pallas_call | solution.py:375
  188.2 5.1 %all-to-all-done.5 = bf16[16,16,768]{2,1,0:T(8,128)(2,1)S(1)} async-done(((bf16[16,16,768]{2,1,0:T(8,128)(2,1)}), bf16[16,16,768]{2,1,0:T(8,128)(2,1)S(1)}, u32[]{:S(2)}, u32[]{:S(2)}) %all-to-all-start.5) | async-done | bytes 393248 | tf_op jit(solution)/shard_map/all_to_all | solution.py:384
  193.3 0.7 copy.16
  (2 shorter events, 0.0 us)
Async XLA Ops:
  7.2 11.2 %copy-start.2 = (bf16[2048,768]{1,0:T(8,128)(2,1)S(1)}, bf16[2048,768]{1,0:T(8,128)(2,1)}, u32[]{:S(2)}) copy-start(bf16[2048,768]{1,0:T(8,128)(2,1)} %points_ref.1) | copy-start | bytes 9437188
  7.2 19.8 %all-to-all-start.3 = ((bf16[16,16,768]{2,1,0:T(8,128)(2,1)}), bf16[16,16,768]{2,1,0:T(8,128)(2,1)S(1)}, u32[]{:S(2)}, u32[]{:S(2)}) async-start(bf16[16,16,768]{2,1,0:T(8,128)(2,1)} %param.10), calls=%async_computation.3 | async-start | bytes 786432 | tf_op jit(solution)/shard_map/all_to_all | solution.py:384
  27.0 0.7 copy-start
  27.7 82.6 %all-to-all-start.2 = ((bf16[32,128,768]{2,1,0:T(8,128)(2,1)}), bf16[32,128,768]{2,1,0:T(8,128)(2,1)}, u32[]{:S(2)}, u32[]{:S(2)}) async-start(bf16[32,128,768]{2,1,0:T(8,128)(2,1)} %bitcast.16), calls=%async_computation.2 | async-start | bytes 12582912 | tf_op jit(solution)/shard_map/all_to_all | solution.py:384
  35.1 78.5 %all-gather.2.cloned.1.call-start = ((), (), s32[]{:S(2)}) async-start(), calls=%async_computation.8 | async-start | bytes 3538944 | tf_op jit(solution)/shard_map/all_gather | solution.py:400
  35.9 140.0 %reduce-scatter.2.cloned.1.call-start = ((), (), s32[]{:S(2)}) async-start(), calls=%async_computation.9 | async-start | bytes 3538944 | tf_op jit(solution)/shard_map/reduce_scatter | solution.py:417
  127.7 48.2 %copy-start.1 = (bf16[16,16,768]{2,1,0:T(8,128)(2,1)S(1)}, bf16[16,16,768]{2,1,0:T(8,128)(2,1)}, u32[]{:S(2)}) copy-start(bf16[16,16,768]{2,1,0:T(8,128)(2,1)} %copy-done) | copy-start | bytes 1179652
  127.7 58.4 %copy-start.3 = (s32[8,2048]{1,0:T(8,128)S(1)}, s32[8,2048]{1,0:T(8,128)}, u32[]{:S(2)}) copy-start(s32[8,2048]{1,0:T(8,128)} %get-tuple-element.25.place_ref) | copy-start | bytes 196612
  129.0 16.3 %all-to-all-start.4 = ((f32[8,1,256]{2,1,0:T(1,128)}), f32[8,1,256]{2,1,0:T(1,128)S(1)}, u32[]{:S(2)}, u32[]{:S(2)}) async-start(f32[8,1,256]{2,1,0:T(1,128)} %copy.8), calls=%async_computation.5 | async-start | bytes 16384 | tf_op jit(solution)/shard_map/all_to_all | solution.py:384
  145.3 32.5 %all-to-all-start.6 = ((f32[32,1,192]{2,1,0:T(1,128)}), f32[32,1,192]{2,1,0:T(1,128)S(1)}, u32[]{:S(2)}, u32[]{:S(2)}) async-start(f32[32,1,192]{2,1,0:T(1,128)} %all_to_all.34), calls=%async_computation.7 | async-start | bytes 65536 | tf_op jit(solution)/shard_map/all_to_all | solution.py:384
  177.8 15.5 %all-to-all-start.5 = ((bf16[16,16,768]{2,1,0:T(8,128)(2,1)}), bf16[16,16,768]{2,1,0:T(8,128)(2,1)S(1)}, u32[]{:S(2)}, u32[]{:S(2)}) async-start(bf16[16,16,768]{2,1,0:T(8,128)(2,1)} %fusion.1), calls=%async_computation.6 | async-start | bytes 786432 | tf_op jit(solution)/shard_map/all_to_all | solution.py:384
Sparse Core Ops, SparseCore 0:
  38.3 47.6 all-gather.1
  127.8 48.0 reduce-scatter.1

commit v5 on v4

--- a/solution.py
+++ b/solution.py
@@ -384,6 +384,14 @@
     return lax.all_to_all(x, axes, split_axis=0, concat_axis=0, tiled=True)
 
 
+def swap_step(x, dim, axis, bit, beside):
+    other = 1 - ((lax.axis_index(axis) >> bit) & 1)
+    send = lax.dynamic_index_in_dim(x, other, dim, keepdims=True)
+    got = lax.ppermute(send, axis, [(i, i ^ (1 << bit)) for i in range(4)])
+    got, beside = lax.optimization_barrier((got, beside))
+    return lax.dynamic_update_index_in_dim(x, got, other, dim), beside
+
+
 def local(points, coarse_id, owner_map, centroids):
     zn, cores = lax.axis_size("z"), lax.axis_size("core")
     dpn = lax.axis_size("y") * lax.axis_size("x")
@@ -391,12 +399,17 @@
     bound = zn * CAP
     rows, width = points.shape
 
-    panel = exchange(centroids, ("y", "x")).reshape(-1, width)
-    place, note, segment = index(
+    block = centroids.reshape((2, 2, 2, 2) + centroids.shape[1:])
+    found = index(
         coarse_id.reshape(1, rows), owner_map.reshape(1, -1), zn, dpn, cores, bound
     )
+    block, (place, note, segment) = swap_step(block, 0, "y", 1, found)
     packed = sort_pack(segment, place, points, note, ROWS, bound, zn, 1024)
+    block, packed = swap_step(block, 2, "x", 1, packed)
     arrived = exchange(packed.reshape(peers, ROWS, width), PLANE)
+    block, _ = swap_step(block, 1, "y", 0, ())
+    block, _ = swap_step(block, 3, "x", 0, ())
+    panel = block.reshape(-1, width)
     panels = lax.all_gather(panel, "z", axis=0)
 
     most = jnp.max(arrived[:, ROWS - 1, zn].astype(F32))

time: 202 us -> 248 us (1.23)
  waiting for transfers between devices: 110 us -> 160 us
  starting transfers between devices: 37.7 us -> 33.1 us
    ppermute x0 -> x4, waiting for transfers between devices: none -> 77.6 us  [swap_step(): got = lax.ppermute(send, axis, [(i, i ^ 1 << bit) for i in range(4)])]
    all_to_all x5 -> x4, waiting for transfers between devices: 85.7 us -> 11.8 us  [exchange(): return lax.all_to_all(x, axes, split_axis=0, concat_axis=0, tiled=True)]
    all_gather x1, waiting for transfers between devices: 0.02 us -> 45.7 us  [local(): panels = lax.all_gather(panel, 'z', axis=0)]
    all_to_all x5 -> x4, starting transfers between devices: 37.6 us -> 25.4 us  [exchange(): return lax.all_to_all(x, axes, split_axis=0, concat_axis=0, tiled=True)]
    ppermute x0 -> x4, starting transfers between devices: none -> 7.56 us  [swap_step(): got = lax.ppermute(send, axis, [(i, i ^ 1 << bit) for i in range(4)])]
  transfers between devices with their start and end apart: 7 -> 10, of which waited for: 4 -> 6; matrix products, arithmetic and copies ran while one was open for 3% -> 3% of each run, Pallas kernels for 7% -> 6%
where the time goes in v5:
time: 248 us
  waiting for transfers between devices  160 us (65%)
  starting transfers between devices  33.1 us (13%)
  Pallas kernels  29.1 us (12%)
  between operations  15.5 us (6%)
  local copies, waits for them, and re-layouts  6.02 us (2%)
  other arithmetic  3.63 us (1%)
    ppermute x4, waiting for transfers between devices, swap_step(): got = lax.ppermute(send, axis, [(i, i ^ 1 << bit) for i in range(4)])  77.6 us
    all_gather x1, waiting for transfers between devices, local(): panels = lax.all_gather(panel, 'z', axis=0)  45.7 us
    all_to_all x4, starting transfers between devices, exchange(): return lax.all_to_all(x, axes, split_axis=0, concat_axis=0, tiled=True)  25.4 us
    reduce_scatter x1, waiting for transfers between devices, local(): sums = lax.psum_scatter(sums, 'z', scatter_dimension=0, tiled=True)[0]  24.9 us
    pallas_call x1, Pallas kernels, assign(): pl.pallas_call(functools.partial(assign_kernel, steps, zn, few, slots), g...  14 us
    all_to_all x4, waiting for transfers between devices, exchange(): return lax.all_to_all(x, axes, split_axis=0, concat_axis=0, tiled=True)  11.8 us
    pallas_call x1, Pallas kernels, sort_pack(): pl.pallas_call(functools.partial(sort_pack_kernel, per, bound, zn), grid_...  9.65 us
    ppermute x4, starting transfers between devices, swap_step(): got = lax.ppermute(send, axis, [(i, i ^ 1 << bit) for i in range(4)])  7.56 us
  transfers between devices with their start and end apart: 10, of which 6 were waited for; matrix products, arithmetic and copies ran while one was open for 3% of the time, Pallas kernels for 6%

profile of v5, /device:TPU:2, one launch (start us, length us, event | category | flops | bytes accessed | tf_op | source)
XLA Modules:
  0.0 247.6 jit_solution(1522603031273863664)
XLA Ops:
  7.2 1.0 copy.21
  8.2 3.3 %collective-permute-start = (bf16[1,2,2,2,16,768]{5,4,3,2,1,0:T(8,128)(2,1)S(1)}, bf16[1,2,2,2,16,768]{5,4,3,2,1,0:T(8,128)(2,1)S(1)}, u32[]{:S(2)}, u32[]{:S(2)}) collective-permute-start(bf16[1,2,2,2,16,768]{5,4,3,2,1,0:T(8,128)(2,1)S(1)} %constant_dynamic-slice_fusion.3), channel_id=1, source_target_pairs={{0,128},{64,192},{128,0},{192,64},{1,129},{65,193},{129,1},{193,65... | collective-permute-start | bytes 589832 | tf_op jit(solution)/shard_map/ppermute | solution.py:390
  11.5 3.4 %place.1 = (s32[8,2048]{1,0:T(8,128)S(1)}, f32[32,128]{1,0:T(8,128)}, s32[8,384]{1,0:T(8,128)}) custom-call(s32[1,2048]{1,0:T(1,128)} %bitcast.31, s32[1,256]{1,0:T(1,128)} %bitcast.32), custom_call_target="tpu_custom_call" | custom-call | flops 1000000000 | bytes 100000 | tf_op jit(solution)/shard_map/place/pallas_call | solution.py:92
  14.8 0.0 copy-start.4
  14.8 1.6 collective-permute-done
  16.5 2.2 collective-permute-start.1
  18.7 9.7 %sort_pack.1 = bf16[4096,768]{1,0:T(8,128)(2,1)} custom-call(s32[8,384]{1,0:T(8,128)} %get-tuple-element.34.segment_ref, s32[8,2048]{1,0:T(8,128)S(1)} %get-tuple-element.35.place_ref, bf16[2048,768]{1,0:T(8,128)(2,1)} %points_ref.1, f32[32,128]{1,0:T(8,128)} %get-tuple-element.36.note_ref), custom_call_target="tpu_custom_call" | custom-call | flops 5000000000 | bytes 10000000 | tf_op jit(solution)/shard_map/sort_pack/pallas_call | solution.py:209
  28.3 0.0 collective-permute-done.1
  28.4 1.7 collective-permute-start.2
  30.1 6.4 %all-to-all-start.2 = ((bf16[32,128,768]{2,1,0:T(8,128)(2,1)}), bf16[32,128,768]{2,1,0:T(8,128)(2,1)}, u32[]{:S(2)}, u32[]{:S(2)}) async-start(bf16[32,128,768]{2,1,0:T(8,128)(2,1)} %bitcast.22), calls=%async_computation.2 | async-start | bytes 12582912 | tf_op jit(solution)/shard_map/all_to_all | solution.py:384
  36.5 0.0 all-gather.2.cloned.1.call-start
  36.5 0.0 collective-permute-done.2
  36.6 0.4 collective-permute-start.3
  37.0 76.0 %collective-permute-done.3 = bf16[2,2,2,1,16,768]{5,4,3,2,1,0:T(8,128)(2,1)S(1)} collective-permute-done((bf16[2,2,2,1,16,768]{5,4,3,2,1,0:T(8,128)(2,1)S(1)}, bf16[2,2,2,1,16,768]{5,4,3,2,1,0:T(8,128)(2,1)S(1)}, u32[]{:S(2)}, u32[]{:S(2)}) %collective-permute-start.3) | collective-permute-done | bytes 196640 | tf_op jit(solution)/shard_map/ppermute | solution.py:390
  113.0 0.0 copy-start
  113.0 0.7 copy-done
  113.8 0.0 all-gather.2.cloned.1.call-update
  113.8 0.0 reduce-scatter.2.cloned.1.call-start
  113.9 0.0 all-to-all-done.2
  113.9 1.6 slice_reduce_fusion
  116.7 0.0 copy-done.4
  116.7 0.5 conditional.1
  116.8 0.2 broadcast.14
  117.2 0.0 copy-start.2
  117.2 45.7 %all-gather.2.cloned.1.call-done.panel_ref = bf16[8,256,768]{2,1,0:T(8,128)(2,1)} async-done(((bf16[1,256,768]{2,1,0:T(8,128)(2,1)}), bf16[8,256,768]{2,1,0:T(8,128)(2,1)}) %all-gather.2.cloned.1.call-update) | async-done | bytes 3145744 | tf_op jit(solution)/shard_map/all_gather | solution.py:413
  163.0 0.0 copy-done.2
  163.0 0.0 copy-start.1
  163.0 14.0 %assign.1 = (bf16[8,256,768]{2,1,0:T(8,128)(2,1)}, f32[8,256]{1,0:T(8,128)}, f32[8,768]{1,0:T(8,128)}) custom-call(s32[1]{0:T(128)} %bitcast.8.flag_ref, bf16[4096,768]{1,0:T(8,128)(2,1)} %bitcast.9.in_ref, bf16[2304,768]{1,0:T(8,128)(2,1)} %copy-done.2, bf16[8,256,768]{2,1,0:T(8,128)(2,1)} %all-gather.2.cloned.1.call-done.panel_ref), custom_call_target="tpu_custom_call" | custom-call | flops 8000000000 | bytes 20000000 | tf_op jit(solution)/shard_map/assign/pallas_call | solution.py:329
  177.0 0.0 copy-start.3
  177.0 0.0 copy-start.5
  177.0 0.0 reduce-scatter.2.cloned.1.call-update
  177.0 1.3 copy.8
  178.3 4.3 %all-to-all-start.3 = ((f32[8,1,256]{2,1,0:T(1,128)}), f32[8,1,256]{2,1,0:T(1,128)S(1)}, u32[]{:S(2)}, u32[]{:S(2)}) async-start(f32[8,1,256]{2,1,0:T(1,128)} %copy.8), calls=%async_computation.4 | async-start | bytes 16384 | tf_op jit(solution)/shard_map/all_to_all | solution.py:384
  182.7 0.0 copy-done.1
  182.7 0.1 convert_multiply_fusion
  182.8 0.0 copy-done.3
  182.8 0.1 reshape.77
  182.9 0.1 copy.9
  183.0 0.8 all_to_all.30
  183.7 6.7 %all-to-all-done.3 = f32[8,1,256]{2,1,0:T(1,128)S(1)} async-done(((f32[8,1,256]{2,1,0:T(1,128)}), f32[8,1,256]{2,1,0:T(1,128)S(1)}, u32[]{:S(2)}, u32[]{:S(2)}) %all-to-all-start.3) | async-done | bytes 8224 | tf_op jit(solution)/shard_map/all_to_all | solution.py:384
  190.4 7.4 %all-to-all-start.5 = ((f32[32,1,192]{2,1,0:T(1,128)}), f32[32,1,192]{2,1,0:T(1,128)S(1)}, u32[]{:S(2)}, u32[]{:S(2)}) async-start(f32[32,1,192]{2,1,0:T(1,128)} %all_to_all.30), calls=%async_computation.6 | async-start | bytes 65536 | tf_op jit(solution)/shard_map/all_to_all | solution.py:384
  197.8 0.1 add.61
  197.9 24.9 %reduce-scatter.2.cloned.1.call-done = bf16[1,256,768]{2,1,0:T(8,128)(2,1)} async-done(((bf16[8,256,768]{2,1,0:T(8,128)(2,1)}), bf16[1,256,768]{2,1,0:T(8,128)(2,1)}) %reduce-scatter.2.cloned.1.call-update) | async-done | bytes 393232 | tf_op jit(solution)/shard_map/reduce_scatter | solution.py:430
  222.8 1.9 fusion.1
  224.7 0.0 all-to-all-done.5
  224.7 7.3 %all-to-all-start.4 = ((bf16[16,16,768]{2,1,0:T(8,128)(2,1)}), bf16[16,16,768]{2,1,0:T(8,128)(2,1)S(1)}, u32[]{:S(2)}, u32[]{:S(2)}) async-start(bf16[16,16,768]{2,1,0:T(8,128)(2,1)} %fusion.1), calls=%async_computation.5 | async-start | bytes 786432 | tf_op jit(solution)/shard_map/all_to_all | solution.py:384
  232.0 0.1 reduce.3
  232.1 0.1 reshape.78
  232.2 0.7 copy.11
  232.9 0.0 copy-done.5
  232.9 2.1 lookup.1
  234.9 5.1 %all-to-all-done.4 = bf16[16,16,768]{2,1,0:T(8,128)(2,1)S(1)} async-done(((bf16[16,16,768]{2,1,0:T(8,128)(2,1)}), bf16[16,16,768]{2,1,0:T(8,128)(2,1)S(1)}, u32[]{:S(2)}, u32[]{:S(2)}) %all-to-all-start.4) | async-done | bytes 393248 | tf_op jit(solution)/shard_map/all_to_all | solution.py:384
  240.0 0.7 copy.22
  (10 shorter events, 0.2 us)
Async XLA Ops:
  8.2 8.2 %collective-permute-start = (bf16[1,2,2,2,16,768]{5,4,3,2,1,0:T(8,128)(2,1)S(1)}, bf16[1,2,2,2,16,768]{5,4,3,2,1,0:T(8,128)(2,1)S(1)}, u32[]{:S(2)}, u32[]{:S(2)}) collective-permute-start(bf16[1,2,2,2,16,768]{5,4,3,2,1,0:T(8,128)(2,1)S(1)} %constant_dynamic-slice_fusion.3), channel_id=1, source_target_pairs={{0,128},{64,192},{128,0},{192,64},{1,129},{65,193},{129,1},{193,65... | collective-permute-start | bytes 589832 | tf_op jit(solution)/shard_map/ppermute | solution.py:390
  14.8 101.9 %copy-start.4 = (s32[8,2048]{1,0:T(8,128)}, s32[8,2048]{1,0:T(8,128)S(1)}, u32[]{:S(2)}) copy-start(s32[8,2048]{1,0:T(8,128)S(1)} %get-tuple-element.35.place_ref) | copy-start | bytes 196612
  16.5 11.9 %collective-permute-start.1 = (bf16[2,2,1,2,16,768]{5,4,3,2,1,0:T(8,128)(2,1)S(1)}, bf16[2,2,1,2,16,768]{5,4,3,2,1,0:T(8,128)(2,1)S(1)}, u32[]{:S(2)}, u32[]{:S(2)}) collective-permute-start(bf16[2,2,1,2,16,768]{5,4,3,2,1,0:T(8,128)(2,1)S(1)} %constant_dynamic-slice_fusion.2), channel_id=1, source_target_pairs={{0,32},{16,48},{32,0},{48,16},{1,33},{17,49},{33,1},{49,17},{2,34}... | collective-permute-start | bytes 589832 | tf_op jit(solution)/shard_map/ppermute | solution.py:390
  28.4 8.1 %collective-permute-start.2 = (bf16[2,1,2,2,16,768]{5,4,3,2,1,0:T(8,128)(2,1)S(1)}, bf16[2,1,2,2,16,768]{5,4,3,2,1,0:T(8,128)(2,1)S(1)}, u32[]{:S(2)}, u32[]{:S(2)}) collective-permute-start(bf16[2,1,2,2,16,768]{5,4,3,2,1,0:T(8,128)(2,1)S(1)} %constant_dynamic-slice_fusion.1), channel_id=1, source_target_pairs={{0,64},{64,0},{128,192},{192,128},{1,65},{65,1},{129,193},{193,129... | collective-permute-start | bytes 589832 | tf_op jit(solution)/shard_map/ppermute | solution.py:390
  30.1 83.8 %all-to-all-start.2 = ((bf16[32,128,768]{2,1,0:T(8,128)(2,1)}), bf16[32,128,768]{2,1,0:T(8,128)(2,1)}, u32[]{:S(2)}, u32[]{:S(2)}) async-start(bf16[32,128,768]{2,1,0:T(8,128)(2,1)} %bitcast.22), calls=%async_computation.2 | async-start | bytes 12582912 | tf_op jit(solution)/shard_map/all_to_all | solution.py:384
  36.5 126.5 %all-gather.2.cloned.1.call-start = ((), (), s32[]{:S(2)}) async-start(), calls=%async_computation.7 | async-start | bytes 3538944 | tf_op jit(solution)/shard_map/all_gather | solution.py:413
  36.6 76.4 %collective-permute-start.3 = (bf16[2,2,2,1,16,768]{5,4,3,2,1,0:T(8,128)(2,1)S(1)}, bf16[2,2,2,1,16,768]{5,4,3,2,1,0:T(8,128)(2,1)S(1)}, u32[]{:S(2)}, u32[]{:S(2)}) collective-permute-start(bf16[2,2,2,1,16,768]{5,4,3,2,1,0:T(8,128)(2,1)S(1)} %constant_dynamic-slice_fusion), channel_id=1, source_target_pairs={{0,16},{16,0},{32,48},{48,32},{1,17},{17,1},{33,49},{49,33},{2,18}... | collective-permute-start | bytes 589832 | tf_op jit(solution)/shard_map/ppermute | solution.py:390
  113.0 0.7 copy-start
  113.8 109.0 %reduce-scatter.2.cloned.1.call-start = ((), (), s32[]{:S(2)}) async-start(), calls=%async_computation.8 | async-start | bytes 3538944 | tf_op jit(solution)/shard_map/reduce_scatter | solution.py:430
  117.2 45.8 %copy-start.2 = (bf16[2304,768]{1,0:T(8,128)(2,1)}, bf16[2304,768]{1,0:T(8,128)(2,1)S(1)}, u32[]{:S(2)}) copy-start(bf16[2304,768]{1,0:T(8,128)(2,1)S(1)} %get-tuple-element.46.more_ref) | copy-start | bytes 10616836
  163.0 19.7 %copy-start.1 = (bf16[2,2,2,2,16,768]{5,4,3,2,1,0:T(8,128)(2,1)S(1)}, bf16[2,2,2,2,16,768]{5,4,3,2,1,0:T(8,128)(2,1)}, u32[]{:S(2)}) copy-start(bf16[2,2,2,2,16,768]{5,4,3,2,1,0:T(8,128)(2,1)} %copy-done) | copy-start | bytes 1179652
  177.0 5.8 %copy-start.3 = (f32[8,768]{1,0:T(8,128)S(1)}, f32[8,768]{1,0:T(8,128)}, u32[]{:S(2)}) copy-start(f32[8,768]{1,0:T(8,128)} %get-tuple-element.41) | copy-start | bytes 73732
  177.0 55.9 %copy-start.5 = (s32[8,2048]{1,0:T(8,128)S(1)}, s32[8,2048]{1,0:T(8,128)}, u32[]{:S(2)}) copy-start(s32[8,2048]{1,0:T(8,128)} %copy-done.4) | copy-start | bytes 196612
  178.3 12.1 %all-to-all-start.3 = ((f32[8,1,256]{2,1,0:T(1,128)}), f32[8,1,256]{2,1,0:T(1,128)S(1)}, u32[]{:S(2)}, u32[]{:S(2)}) async-start(f32[8,1,256]{2,1,0:T(1,128)} %copy.8), calls=%async_computation.4 | async-start | bytes 16384 | tf_op jit(solution)/shard_map/all_to_all | solution.py:384
  190.4 34.3 %all-to-all-start.5 = ((f32[32,1,192]{2,1,0:T(1,128)}), f32[32,1,192]{2,1,0:T(1,128)S(1)}, u32[]{:S(2)}, u32[]{:S(2)}) async-start(f32[32,1,192]{2,1,0:T(1,128)} %all_to_all.30), calls=%async_computation.6 | async-start | bytes 65536 | tf_op jit(solution)/shard_map/all_to_all | solution.py:384
  224.7 15.3 %all-to-all-start.4 = ((bf16[16,16,768]{2,1,0:T(8,128)(2,1)}), bf16[16,16,768]{2,1,0:T(8,128)(2,1)S(1)}, u32[]{:S(2)}, u32[]{:S(2)}) async-start(bf16[16,16,768]{2,1,0:T(8,128)(2,1)} %fusion.1), calls=%async_computation.5 | async-start | bytes 786432 | tf_op jit(solution)/shard_map/all_to_all | solution.py:384
Sparse Core Ops, SparseCore 0:
  113.9 48.9 all-gather.1
  177.1 45.6 reduce-scatter.1
